TPU v7x, 32 devices: a whole 2x2x4 slice. The times are simulated.
32 devices in a mesh: wide: 8 (over y, x, core), narrow: 4 (over z).
Axes of the slice: x: 2, y: 2, z: 4, core: 2. Of those that a mesh axis runs over, the one named last changes fastest.
Arguments:
- latents: bfloat16 [2, 32, 16, 16, 768], P(None, ('wide', 'narrow')), may hold values from -6 to 6
- buckets: int32 [2, 32], P(None, ('wide', 'narrow')), may hold values from 0 to 2
- step_ids: int32 [2, 32], P(None, ('wide', 'narrow')), may hold values from 0 to 999
- qkv_spatial: bfloat16 [1769472], P(('wide', 'narrow')), may hold values from -0.21875 to 0.21875
- proj_spatial: bfloat16 [589824], P(('wide', 'narrow')), may hold values from -0.625 to 0.625
- qkv_temporal: bfloat16 [1769472], P(('wide', 'narrow')), may hold values from -0.21875 to 0.21875
- proj_temporal: bfloat16 [589824], P(('wide', 'narrow')), may hold values from -0.4375 to 0.4375
- up_weight: bfloat16 [2359296], P(('wide', 'narrow')), may hold values from -0.21875 to 0.21875
- down_weight: bfloat16 [2359296], P(('wide', 'narrow')), may hold values from -0.109375 to 0.109375
- ada_weight: bfloat16 [5308416], P(('wide', 'narrow')), may hold values from -0.21875 to 0.21875
- biases: bfloat16 [10752], P(('wide', 'narrow')), may hold values from -3 to 3
- cotangent: bfloat16 [2, 32, 16, 16, 768], P(None, ('wide', 'narrow')), may hold values from -6 to 6
Outputs:
- output: bfloat16 [2, 32, 16, 16, 768], P(None, ('wide', 'narrow'))
- latents_grad: float32 [2, 32, 16, 16, 768], P(None, ('wide', 'narrow'))
- qkv_spatial_grad: float32 [1769472], P(('wide', 'narrow'))
- proj_spatial_grad: float32 [589824], P(('wide', 'narrow'))
- qkv_temporal_grad: float32 [1769472], P(('wide', 'narrow'))
- proj_temporal_grad: float32 [589824], P(('wide', 'narrow'))
- up_weight_grad: float32 [2359296], P(('wide', 'narrow'))
- down_weight_grad: float32 [2359296], P(('wide', 'narrow'))
- ada_weight_grad: float32 [5308416], P(('wide', 'narrow'))
- biases_grad: float32 [10752], P(('wide', 'narrow'))
Inputs may be any that keep to these rules, and one draw needn't show every extreme that they name: `buckets`: an item's bucket sets how many leading spatial positions of each of its frames hold data: 16, 8 or 2 for 0, 1 or 2.
All inputs are finite; a program needn't handle non-finite values.
Results may differ from a plain program's by a relative error of at most 0.02.
Values may be sent and summed in bfloat16 or wider, within the bound.
A program may use at most 320 MiB of HBM per device.

v0:
```python
from functools import partial
import math

import jax
import jax.numpy as jnp
from jax import lax
from jax.sharding import PartitionSpec as P

D = 768
HEADS = 12
HD = 64
FF = 3072


epsilon = 1e-06
masked_score = -1e30


def collect_forward(shards):
    return (
        lax.all_gather(shards[0], ("wide", "narrow"), axis=0, tiled=True),
        lax.all_gather(shards[1], ("wide", "narrow"), axis=0, tiled=True),
        lax.all_gather(shards[2], ("wide", "narrow"), axis=0, tiled=True),
        lax.all_gather(shards[3], ("wide", "narrow"), axis=0, tiled=True),
        lax.all_gather(shards[4], ("wide", "narrow"), axis=0, tiled=True),
        lax.all_gather(shards[5], ("wide", "narrow"), axis=0, tiled=True),
        lax.all_gather(shards[6], ("wide", "narrow"), axis=0, tiled=True),
        lax.all_gather(shards[7], ("wide", "narrow"), axis=0, tiled=True),
    )


def collect_backward(shards):
    return (
        lax.all_gather(shards[0], ("wide", "narrow"), axis=0, tiled=True),
        lax.all_gather(shards[1], ("wide", "narrow"), axis=0, tiled=True),
        lax.all_gather(shards[2], ("wide", "narrow"), axis=0, tiled=True),
        lax.all_gather(shards[3], ("wide", "narrow"), axis=0, tiled=True),
        lax.all_gather(shards[4], ("wide", "narrow"), axis=0, tiled=True),
        lax.all_gather(shards[5], ("wide", "narrow"), axis=0, tiled=True),
        lax.all_gather(shards[6], ("wide", "narrow"), axis=0, tiled=True),
        lax.all_gather(shards[7], ("wide", "narrow"), axis=0, tiled=True),
    )


def spread(gradients):
    outer = lax.axis_size("wide")
    inner = lax.axis_size("narrow")
    shaped = tuple((grad.reshape(outer, inner, -1) for grad in gradients))
    arrived = (
        lax.all_to_all(
            lax.all_to_all(
                shaped[0].astype(jnp.bfloat16), "wide", split_axis=0, concat_axis=0, tiled=True
            ),
            "narrow",
            split_axis=1,
            concat_axis=1,
            tiled=True,
        ).astype(jnp.float32),
        lax.all_to_all(
            lax.all_to_all(
                shaped[1].astype(jnp.bfloat16), "wide", split_axis=0, concat_axis=0, tiled=True
            ),
            "narrow",
            split_axis=1,
            concat_axis=1,
            tiled=True,
        ).astype(jnp.float32),
        lax.all_to_all(
            lax.all_to_all(
                shaped[2].astype(jnp.bfloat16), "wide", split_axis=0, concat_axis=0, tiled=True
            ),
            "narrow",
            split_axis=1,
            concat_axis=1,
            tiled=True,
        ).astype(jnp.float32),
        lax.all_to_all(
            lax.all_to_all(
                shaped[3].astype(jnp.bfloat16), "wide", split_axis=0, concat_axis=0, tiled=True
            ),
            "narrow",
            split_axis=1,
            concat_axis=1,
            tiled=True,
        ).astype(jnp.float32),
        lax.all_to_all(
            lax.all_to_all(
                shaped[4].astype(jnp.bfloat16), "wide", split_axis=0, concat_axis=0, tiled=True
            ),
            "narrow",
            split_axis=1,
            concat_axis=1,
            tiled=True,
        ).astype(jnp.float32),
        lax.all_to_all(
            lax.all_to_all(
                shaped[5].astype(jnp.bfloat16), "wide", split_axis=0, concat_axis=0, tiled=True
            ),
            "narrow",
            split_axis=1,
            concat_axis=1,
            tiled=True,
        ).astype(jnp.float32),
        lax.all_to_all(
            lax.all_to_all(
                shaped[6].astype(jnp.bfloat16), "wide", split_axis=0, concat_axis=0, tiled=True
            ),
            "narrow",
            split_axis=1,
            concat_axis=1,
            tiled=True,
        ).astype(jnp.float32),
        lax.all_to_all(
            lax.all_to_all(
                shaped[7].astype(jnp.bfloat16), "wide", split_axis=0, concat_axis=0, tiled=True
            ),
            "narrow",
            split_axis=1,
            concat_axis=1,
            tiled=True,
        ).astype(jnp.float32),
    )
    return tuple((jnp.sum(piece, axis=(0, 1)) for piece in arrived))


def unpack(flat_tuple):
    return (
        flat_tuple[0].reshape(D, 3 * D),
        flat_tuple[1].reshape(D, D),
        flat_tuple[2].reshape(D, 3 * D),
        flat_tuple[3].reshape(D, D),
        flat_tuple[4].reshape(D, FF),
        flat_tuple[5].reshape(FF, D),
        flat_tuple[6].reshape(D, 9 * D),
        flat_tuple[7],
    )


def timestep_condition(step_value):
    half_width = D // 2
    frequency = jnp.exp(-math.log(10000.0) * jnp.arange(half_width, dtype=jnp.float32) / half_width)
    angles = step_value.astype(jnp.float32) * frequency
    return jax.nn.silu(jnp.concatenate([jnp.cos(angles), jnp.sin(angles)]))


def modulate(token_rows, shift_row, scale_row):
    centre = token_rows - jnp.mean(token_rows, axis=-1, keepdims=True)
    inverse = lax.rsqrt(jnp.mean(centre * centre, axis=-1, keepdims=True) + epsilon)
    normed = centre * inverse
    return (normed, inverse, (normed * (1.0 + scale_row) + shift_row).astype(jnp.bfloat16))


def modulate_back(pre_grad, normed, inverse, scale_row):
    shift_grad = jnp.sum(pre_grad, axis=(0, 1))
    scale_grad = jnp.sum(pre_grad * normed, axis=(0, 1))
    normed_grad = pre_grad * (1.0 + scale_row)
    rows_grad = inverse * (
        normed_grad
        - jnp.mean(normed_grad, axis=-1, keepdims=True)
        - normed * jnp.mean(normed_grad * normed, axis=-1, keepdims=True)
    )
    return (rows_grad, shift_grad, scale_grad)


def split_heads(projected):
    leading, length = (projected.shape[0], projected.shape[1])
    pieces = projected.reshape(leading, length, 3, HEADS, HD)
    return (pieces[:, :, 0], pieces[:, :, 1], pieces[:, :, 2])


def attention_scores(queries, key_rows, key_valid):
    scores = jnp.einsum(
        "blhd,bmhd->bhlm", queries, key_rows, preferred_element_type=jnp.float32
    ) * HD ** (-0.5)
    if key_valid is not None:
        scores = jnp.where(key_valid[None, None, None, :] > 0.5, scores, masked_score)
    return scores


def attend_forward(normed_low, qkv_matrix, proj_matrix, key_valid):
    leading, length = (normed_low.shape[0], normed_low.shape[1])
    projected = jnp.dot(normed_low, qkv_matrix, preferred_element_type=jnp.float32).astype(
        jnp.bfloat16
    )
    queries, key_rows, values = split_heads(projected)
    scores = attention_scores(queries, key_rows, key_valid)
    row_max = jnp.max(scores, axis=-1, keepdims=True)
    expanded = jnp.exp(scores - row_max)
    totals = jnp.sum(expanded, axis=-1, keepdims=True)
    log_total = row_max + jnp.log(totals)
    soft_low = (expanded / totals).astype(jnp.bfloat16)
    context = jnp.einsum("bhlm,bmhd->blhd", soft_low, values, preferred_element_type=jnp.float32)
    context = context.astype(jnp.bfloat16).reshape(leading, length, D)
    result = jnp.dot(context, proj_matrix, preferred_element_type=jnp.float32)
    return (result, (projected, log_total, context))


def attend_backward(result_grad_low, normed_low, qkv_matrix, proj_matrix, key_valid, kept_state):
    projected, log_total, context = kept_state
    leading, length = (normed_low.shape[0], normed_low.shape[1])
    proj_grad = jnp.einsum(
        "bld,ble->de", context, result_grad_low, preferred_element_type=jnp.float32
    )
    context_grad = jnp.einsum(
        "ble,de->bld", result_grad_low, proj_matrix, preferred_element_type=jnp.float32
    )
    context_grad = context_grad.astype(jnp.bfloat16).reshape(leading, length, HEADS, HD)
    queries, key_rows, values = split_heads(projected)
    soft_full = jnp.exp(attention_scores(queries, key_rows, key_valid) - log_total)
    value_grad = jnp.einsum(
        "bhlm,blhd->bmhd",
        soft_full.astype(jnp.bfloat16),
        context_grad,
        preferred_element_type=jnp.float32,
    )
    soft_grad = jnp.einsum(
        "blhd,bmhd->bhlm", context_grad, values, preferred_element_type=jnp.float32
    )
    row_dot = jnp.sum(soft_grad * soft_full, axis=-1, keepdims=True)
    score_grad = (soft_full * (soft_grad - row_dot)).astype(jnp.bfloat16)
    query_grad = jnp.einsum(
        "bhlm,bmhd->blhd", score_grad, key_rows, preferred_element_type=jnp.float32
    ) * HD ** (-0.5)
    key_grad = jnp.einsum(
        "bhlm,blhd->bmhd", score_grad, queries, preferred_element_type=jnp.float32
    ) * HD ** (-0.5)
    projected_grad = (
        jnp.stack([query_grad, key_grad, value_grad], axis=2)
        .reshape(leading, length, 3 * D)
        .astype(jnp.bfloat16)
    )
    qkv_grad = jnp.einsum(
        "bld,ble->de", normed_low, projected_grad, preferred_element_type=jnp.float32
    )
    normed_grad = jnp.einsum(
        "ble,de->bld", projected_grad, qkv_matrix, preferred_element_type=jnp.float32
    )
    return (normed_grad, qkv_grad, proj_grad)


def item_forward(latent, step_value, valid_mask, matrices):
    space_qkv, space_proj, time_qkv, time_proj, up_matrix, down_matrix, ada_matrix, bias_vector = (
        matrices
    )
    condition = timestep_condition(step_value).astype(jnp.bfloat16)
    modulation = jnp.dot(condition[None, :], ada_matrix, preferred_element_type=jnp.float32)[0]
    modulation = (modulation + bias_vector[: 9 * D].astype(jnp.float32)).reshape(9, D)
    latent_rows = latent.astype(jnp.float32)
    normed_one, inverse_one, low_one = modulate(latent_rows, modulation[0], modulation[1])
    space_out, space_saved = attend_forward(low_one, space_qkv, space_proj, valid_mask)
    after_space = latent_rows + modulation[2] * space_out
    normed_two, inverse_two, low_two = modulate(after_space, modulation[3], modulation[4])
    across = jnp.swapaxes(low_two, 0, 1)
    time_result, time_saved = attend_forward(across, time_qkv, time_proj, None)
    time_out = jnp.swapaxes(time_result, 0, 1)
    after_time = after_space + modulation[5] * time_out
    normed_three, inverse_three, low_three = modulate(after_time, modulation[6], modulation[7])
    hidden = jnp.dot(low_three, up_matrix, preferred_element_type=jnp.float32) + bias_vector[
        9 * D : 9 * D + FF
    ].astype(jnp.float32)
    activated = jax.nn.gelu(hidden, approximate=True).astype(jnp.bfloat16)
    branch = jnp.dot(activated, down_matrix, preferred_element_type=jnp.float32) + bias_vector[
        9 * D + FF :
    ].astype(jnp.float32)
    after_mlp = after_time + modulation[8] * branch
    output = (after_mlp * valid_mask[None, :, None]).astype(jnp.bfloat16)
    kept_state = (
        condition,
        modulation,
        normed_one,
        inverse_one,
        low_one,
        space_out,
        space_saved,
        normed_two,
        inverse_two,
        across,
        time_out,
        time_saved,
        normed_three,
        inverse_three,
        low_three,
        hidden,
        activated,
        branch,
    )
    return (output, kept_state)


def item_backward(grad_low, valid_mask, matrices, kept_state):
    space_qkv, space_proj, time_qkv, time_proj, up_matrix, down_matrix, ada_matrix, bias_vector = (
        matrices
    )
    (
        condition,
        modulation,
        normed_one,
        inverse_one,
        low_one,
        space_out,
        space_saved,
        normed_two,
        inverse_two,
        across,
        time_out,
        time_saved,
        normed_three,
        inverse_three,
        low_three,
        hidden,
        activated,
        branch,
    ) = kept_state
    grad_mlp = grad_low.astype(jnp.float32) * valid_mask[None, :, None]
    branch_grad = (modulation[8] * grad_mlp).astype(jnp.bfloat16)
    gate_three = jnp.sum(grad_mlp * branch, axis=(0, 1))
    down_bias = jnp.sum(branch_grad.astype(jnp.float32), axis=(0, 1))
    down_grad = jnp.einsum(
        "fsk,fsd->kd", activated, branch_grad, preferred_element_type=jnp.float32
    )
    activated_grad = jnp.einsum(
        "fsd,kd->fsk", branch_grad, down_matrix, preferred_element_type=jnp.float32
    )
    gelu_pull = jax.vjp(partial(jax.nn.gelu, approximate=True), hidden)[1]
    hidden_grad = gelu_pull(activated_grad)[0].astype(jnp.bfloat16)
    up_bias = jnp.sum(hidden_grad.astype(jnp.float32), axis=(0, 1))
    up_grad = jnp.einsum("fsd,fsk->dk", low_three, hidden_grad, preferred_element_type=jnp.float32)
    pre_grad = jnp.einsum("fsk,dk->fsd", hidden_grad, up_matrix, preferred_element_type=jnp.float32)
    rows_grad, shift_three, scale_three = modulate_back(
        pre_grad, normed_three, inverse_three, modulation[7]
    )
    grad_time = grad_mlp + rows_grad
    time_grad_low = jnp.swapaxes((modulation[5] * grad_time).astype(jnp.bfloat16), 0, 1)
    gate_two = jnp.sum(grad_time * time_out, axis=(0, 1))
    normed_grad, time_qkv_grad, time_proj_grad = attend_backward(
        time_grad_low, across, time_qkv, time_proj, None, time_saved
    )
    rows_grad, shift_two, scale_two = modulate_back(
        jnp.swapaxes(normed_grad, 0, 1), normed_two, inverse_two, modulation[4]
    )
    grad_space = grad_time + rows_grad
    space_grad_low = (modulation[2] * grad_space).astype(jnp.bfloat16)
    gate_one = jnp.sum(grad_space * space_out, axis=(0, 1))
    normed_grad, space_qkv_grad, space_proj_grad = attend_backward(
        space_grad_low, low_one, space_qkv, space_proj, valid_mask, space_saved
    )
    rows_grad, shift_one, scale_one = modulate_back(
        normed_grad, normed_one, inverse_one, modulation[1]
    )
    latent_grad = grad_space + rows_grad
    modulation_grad = jnp.concatenate(
        [
            shift_one,
            scale_one,
            gate_one,
            shift_two,
            scale_two,
            gate_two,
            shift_three,
            scale_three,
            gate_three,
        ]
    )
    ada_grad = condition.astype(jnp.float32)[:, None] * modulation_grad[None, :]
    bias_grad = jnp.concatenate([modulation_grad, up_bias, down_bias])
    gradients = (
        space_qkv_grad.reshape(-1),
        space_proj_grad.reshape(-1),
        time_qkv_grad.reshape(-1),
        time_proj_grad.reshape(-1),
        up_grad.reshape(-1),
        down_grad.reshape(-1),
        ada_grad.reshape(-1),
        bias_grad,
    )
    return (latent_grad, gradients)


def per_device(
    latents,
    buckets,
    step_ids,
    qkv_spatial,
    proj_spatial,
    qkv_temporal,
    proj_temporal,
    up_weight,
    down_weight,
    ada_weight,
    biases,
    cotangent,
):
    shards = (
        qkv_spatial,
        proj_spatial,
        qkv_temporal,
        proj_temporal,
        up_weight,
        down_weight,
        ada_weight,
        biases,
    )
    spatial_size = latents.shape[3]
    positions = jnp.arange(spatial_size)
    owner_grads = tuple((jnp.zeros(shard.shape, jnp.float32) for shard in shards))
    output_rows = []
    grad_rows = []
    for micro_index in range(latents.shape[0]):
        gathered = collect_forward(shards)
        forward_matrices = unpack(gathered)
        item_index = 0
        bucket = buckets[micro_index, item_index]
        length = jnp.where(
            bucket == 0, spatial_size, jnp.where(bucket == 1, spatial_size // 2, spatial_size // 8)
        )
        valid_mask = (positions < length).astype(jnp.float32)
        output, kept_state = item_forward(
            latents[micro_index, item_index],
            step_ids[micro_index, item_index],
            valid_mask,
            forward_matrices,
        )
        item_outputs = [output]
        item_states = [kept_state]
        item_masks = [valid_mask]
        backward_matrices = unpack(collect_backward(shards))
        micro_grads = None
        item_index = 0
        latent_grad, item_grads = item_backward(
            cotangent[micro_index, item_index],
            item_masks[item_index],
            backward_matrices,
            item_states[item_index],
        )
        item_grads_rows = [latent_grad]
        micro_grads = item_grads
        output_rows.append(jnp.stack(item_outputs))
        grad_rows.append(jnp.stack(item_grads_rows))
        owner_grads = jax.tree.map(jnp.add, owner_grads, spread(micro_grads))
    return (
        jnp.stack(output_rows),
        jnp.stack(grad_rows),
        owner_grads[0],
        owner_grads[1],
        owner_grads[2],
        owner_grads[3],
        owner_grads[4],
        owner_grads[5],
        owner_grads[6],
        owner_grads[7],
    )


def solution(mesh):
    placed = (
        P(None, ("wide", "narrow"), None, None, None),
        P(None, ("wide", "narrow")),
        P(None, ("wide", "narrow")),
        P(("wide", "narrow")),
        P(("wide", "narrow")),
        P(("wide", "narrow")),
        P(("wide", "narrow")),
        P(("wide", "narrow")),
        P(("wide", "narrow")),
        P(("wide", "narrow")),
        P(("wide", "narrow")),
        P(None, ("wide", "narrow"), None, None, None),
    )
    return jax.shard_map(
        per_device,
        mesh=mesh,
        in_specs=placed,
        out_specs=(
            P(None, ("wide", "narrow"), None, None, None),
            P(None, ("wide", "narrow"), None, None, None),
            P(("wide", "narrow")),
            P(("wide", "narrow")),
            P(("wide", "narrow")),
            P(("wide", "narrow")),
            P(("wide", "narrow")),
            P(("wide", "narrow")),
            P(("wide", "narrow")),
            P(("wide", "narrow")),
        ),
        check_vma=False,
    )
```

profile of v0, /device:TPU:0, one launch (start us, length us, event | category | flops | bytes accessed | tf_op | source)
XLA Modules:
  0.0 2861.3 jit_solution(16289556734602304573)
XLA Ops:
  19.6 42.4 %all-reduce = bf16[10752]{0:T(1024)(128)(2,1)S(1)} all-reduce(bf16[10752]{0:T(1024)(128)(2,1)S(1)} %dynamic-update-slice), channel_id=1, replica_groups=mesh['wide'=8,'narrow'=4] {'wide','narrow'}, use_global_device_ids=true, to_apply=%add | all-reduce | flops 10752 | bytes 43008
  70.3 53.2 %all-gather.16.cloned.1.call-done = bf16[589824]{0:T(1024)(128)(2,1)} async-done(((bf16[18432]{0:T(1024)(128)(2,1)}), bf16[589824]{0:T(1024)(128)(2,1)}) %all-gather.16.cloned.1.call-update) | async-done | bytes 1179664 | tf_op jit(solution)/shard_map/all_gather | solution.py:24
  126.9 58.4 %all-gather.10.cloned.1.call-done = bf16[1769472]{0:T(1024)(128)(2,1)} async-done(((bf16[55296]{0:T(1024)(128)(2,1)}), bf16[1769472]{0:T(1024)(128)(2,1)}) %all-gather.10.cloned.1.call-update) | async-done | bytes 3538960 | tf_op jit(solution)/shard_map/all_gather | solution.py:21
  192.9 53.9 %all-gather.14.cloned.1.call-done = bf16[1769472]{0:T(1024)(128)(2,1)} async-done(((bf16[55296]{0:T(1024)(128)(2,1)}), bf16[1769472]{0:T(1024)(128)(2,1)}) %all-gather.14.cloned.1.call-update) | async-done | bytes 3538960 | tf_op jit(solution)/shard_map/all_gather | solution.py:23
  254.4 57.4 %all-gather.18.cloned.1.call-done = bf16[2359296]{0:T(1024)(128)(2,1)} async-done(((bf16[73728]{0:T(1024)(128)(2,1)}), bf16[2359296]{0:T(1024)(128)(2,1)}) %all-gather.18.cloned.1.call-update) | async-done | bytes 4718608 | tf_op jit(solution)/shard_map/all_gather | solution.py:25
  320.0 56.4 %all-gather.20.cloned.1.call-done = bf16[2359296]{0:T(1024)(128)(2,1)} async-done(((bf16[73728]{0:T(1024)(128)(2,1)}), bf16[2359296]{0:T(1024)(128)(2,1)}) %all-gather.20.cloned.1.call-update) | async-done | bytes 4718608 | tf_op jit(solution)/shard_map/all_gather | solution.py:26
  385.7 78.8 %all-gather.8.cloned.1.call-done = bf16[5308416]{0:T(1024)(128)(2,1)} async-done(((bf16[165888]{0:T(1024)(128)(2,1)}), bf16[5308416]{0:T(1024)(128)(2,1)}) %all-gather.8.cloned.1.call-update) | async-done | bytes 10616848 | tf_op jit(solution)/shard_map/all_gather | solution.py:27
  464.5 19.7 reshape.531
  812.8 24.1 all-to-all-done.15
  843.4 25.1 all-to-all-done.7
  875.0 25.1 all-to-all-done.13
  949.5 30.4 %all-to-all-done.10 = bf16[8,4,55296]{2,1,0:T(4,128)(2,1)S(1)} async-done(((bf16[8,4,55296]{2,1,0:T(4,128)(2,1)}), bf16[8,4,55296]{2,1,0:T(4,128)(2,1)S(1)}, u32[]{:S(2)}, u32[]{:S(2)}) %all-to-all-start.10) | async-done | bytes 3538976 | tf_op jit(solution)/shard_map/all_to_all | solution.py:69
  993.6 34.6 %all-to-all-done.8 = bf16[8,4,55296]{2,1,0:T(4,128)(2,1)} async-done(((bf16[8,4,55296]{2,1,0:T(4,128)(2,1)}), bf16[8,4,55296]{2,1,0:T(4,128)(2,1)}, u32[]{:S(2)}, u32[]{:S(2)}) %all-to-all-start.8) | async-done | bytes 3538976 | tf_op jit(solution)/shard_map/all_to_all | solution.py:69
  1043.6 30.2 %all-to-all-done.2 = bf16[8,4,55296]{2,1,0:T(4,128)(2,1)S(1)} async-done(((bf16[8,4,55296]{2,1,0:T(4,128)(2,1)}), bf16[8,4,55296]{2,1,0:T(4,128)(2,1)S(1)}, u32[]{:S(2)}, u32[]{:S(2)}) %all-to-all-start.2) | async-done | bytes 3538976 | tf_op jit(solution)/shard_map/all_to_all | solution.py:51
  1094.0 27.2 all-to-all-done
  1141.6 40.7 %all-to-all-done.22 = bf16[8,4,73728]{2,1,0:T(4,128)(2,1)} async-done(((bf16[8,4,73728]{2,1,0:T(4,128)(2,1)}), bf16[8,4,73728]{2,1,0:T(4,128)(2,1)}, u32[]{:S(2)}, u32[]{:S(2)}) %all-to-all-start.22) | async-done | bytes 4718624 | tf_op jit(solution)/shard_map/all_to_all | solution.py:96
  1200.8 40.9 %all-to-all-done.18 = bf16[8,4,73728]{2,1,0:T(4,128)(2,1)} async-done(((bf16[8,4,73728]{2,1,0:T(4,128)(2,1)}), bf16[8,4,73728]{2,1,0:T(4,128)(2,1)}, u32[]{:S(2)}, u32[]{:S(2)}) %all-to-all-start.18) | async-done | bytes 4718624 | tf_op jit(solution)/shard_map/all_to_all | solution.py:87
  1258.4 42.6 %all-to-all-done.20 = bf16[8,4,73728]{2,1,0:T(4,128)(2,1)} async-done(((bf16[8,4,73728]{2,1,0:T(4,128)(2,1)}), bf16[8,4,73728]{2,1,0:T(4,128)(2,1)}, u32[]{:S(2)}, u32[]{:S(2)}) %all-to-all-start.20) | async-done | bytes 4718624 | tf_op jit(solution)/shard_map/all_to_all | solution.py:96
  1309.4 51.0 %all-to-all-done.16 = bf16[8,4,73728]{2,1,0:T(4,128)(2,1)} async-done(((bf16[8,4,73728]{2,1,0:T(4,128)(2,1)}), bf16[8,4,73728]{2,1,0:T(4,128)(2,1)}, u32[]{:S(2)}, u32[]{:S(2)}) %all-to-all-start.16) | async-done | bytes 4718624 | tf_op jit(solution)/shard_map/all_to_all | solution.py:87
  1369.9 70.7 %all-to-all-done.11 = bf16[8,4,55296]{2,0,1:T(8,128)(2,1)S(1)} async-done(((bf16[8,4,55296]{2,0,1:T(8,128)(2,1)}), bf16[8,4,55296]{2,0,1:T(8,128)(2,1)S(1)}, u32[]{:S(2)}, u32[]{:S(2)}) %all-to-all-start.11) | async-done | bytes 3538976 | tf_op jit(solution)/shard_map/all_to_all | solution.py:68
  1451.6 72.8 %all-to-all-done.9 = bf16[8,4,55296]{2,0,1:T(8,128)(2,1)} async-done(((bf16[8,4,55296]{2,0,1:T(8,128)(2,1)}), bf16[8,4,55296]{2,0,1:T(8,128)(2,1)}, u32[]{:S(2)}, u32[]{:S(2)}) %all-to-all-start.9) | async-done | bytes 3538976 | tf_op jit(solution)/shard_map/all_to_all | solution.py:68
  1542.0 20.9 mul.884
  1571.5 20.9 mul.899
  1627.9 63.5 %all-to-all-done.1 = bf16[8,4,55296]{2,0,1:T(8,128)(2,1)} async-done(((bf16[8,4,55296]{2,0,1:T(8,128)(2,1)}), bf16[8,4,55296]{2,0,1:T(8,128)(2,1)}, u32[]{:S(2)}, u32[]{:S(2)}) %all-to-all-start.1) | async-done | bytes 3538976 | tf_op jit(solution)/shard_map/all_to_all | solution.py:50
  1708.9 105.5 %all-to-all-done.24 = bf16[8,4,165888]{2,1,0:T(4,128)(2,1)} async-done(((bf16[8,4,165888]{2,1,0:T(4,128)(2,1)}), bf16[8,4,165888]{2,1,0:T(4,128)(2,1)}, u32[]{:S(2)}, u32[]{:S(2)}) %all-to-all-start.24) | async-done | bytes 10616864 | tf_op jit(solution)/shard_map/all_to_all | solution.py:105
  1827.0 110.8 %all-to-all-done.26 = bf16[8,4,165888]{2,1,0:T(4,128)(2,1)} async-done(((bf16[8,4,165888]{2,1,0:T(4,128)(2,1)}), bf16[8,4,165888]{2,1,0:T(4,128)(2,1)}, u32[]{:S(2)}, u32[]{:S(2)}) %all-to-all-start.26) | async-done | bytes 10616864 | tf_op jit(solution)/shard_map/all_to_all | solution.py:105
  1949.8 94.7 %all-to-all-done.23 = bf16[8,4,73728]{2,0,1:T(8,128)(2,1)} async-done(((bf16[8,4,73728]{2,0,1:T(8,128)(2,1)}), bf16[8,4,73728]{2,0,1:T(8,128)(2,1)}, u32[]{:S(2)}, u32[]{:S(2)}) %all-to-all-start.23) | async-done | bytes 4718624 | tf_op jit(solution)/shard_map/all_to_all | solution.py:95
  2056.6 96.8 %all-to-all-done.19 = bf16[8,4,73728]{2,0,1:T(8,128)(2,1)} async-done(((bf16[8,4,73728]{2,0,1:T(8,128)(2,1)}), bf16[8,4,73728]{2,0,1:T(8,128)(2,1)}, u32[]{:S(2)}, u32[]{:S(2)}) %all-to-all-start.19) | async-done | bytes 4718624 | tf_op jit(solution)/shard_map/all_to_all | solution.py:86
  2165.5 96.9 %all-to-all-done.21 = bf16[8,4,73728]{2,0,1:T(8,128)(2,1)} async-done(((bf16[8,4,73728]{2,0,1:T(8,128)(2,1)}), bf16[8,4,73728]{2,0,1:T(8,128)(2,1)}, u32[]{:S(2)}, u32[]{:S(2)}) %all-to-all-start.21) | async-done | bytes 4718624 | tf_op jit(solution)/shard_map/all_to_all | solution.py:95
  2279.1 92.2 %all-to-all-done.17 = bf16[8,4,73728]{2,0,1:T(8,128)(2,1)} async-done(((bf16[8,4,73728]{2,0,1:T(8,128)(2,1)}), bf16[8,4,73728]{2,0,1:T(8,128)(2,1)}, u32[]{:S(2)}, u32[]{:S(2)}) %all-to-all-start.17) | async-done | bytes 4718624 | tf_op jit(solution)/shard_map/all_to_all | solution.py:86
  2389.1 218.7 %all-to-all-done.25 = bf16[8,4,165888]{2,0,1:T(8,128)(2,1)} async-done(((bf16[8,4,165888]{2,0,1:T(8,128)(2,1)}), bf16[8,4,165888]{2,0,1:T(8,128)(2,1)}, u32[]{:S(2)}, u32[]{:S(2)}) %all-to-all-start.25) | async-done | bytes 10616864 | tf_op jit(solution)/shard_map/all_to_all | solution.py:104
  2660.8 183.6 %all-to-all-done.27 = bf16[8,4,165888]{2,0,1:T(8,128)(2,1)} async-done(((bf16[8,4,165888]{2,0,1:T(8,128)(2,1)}), bf16[8,4,165888]{2,0,1:T(8,128)(2,1)}, u32[]{:S(2)}, u32[]{:S(2)}) %all-to-all-start.27) | async-done | bytes 10616864 | tf_op jit(solution)/shard_map/all_to_all | solution.py:104
  (734 shorter events, 799.8 us)
Async XLA Ops:
  7.2 60.6 %all-gather.12.cloned.1.call-start = ((), (), s32[]{:S(2)}) async-start(), calls=%async_computation.34 | async-start | bytes 1216512 | tf_op jit(solution)/shard_map/all_gather | solution.py:22
  7.9 115.6 %all-gather.16.cloned.1.call-start = ((), (), s32[]{:S(2)}) async-start(), calls=%async_computation.36 | async-start | bytes 1216512 | tf_op jit(solution)/shard_map/all_gather | solution.py:24
  8.7 176.6 %all-gather.10.cloned.1.call-start = ((), (), s32[]{:S(2)}) async-start(), calls=%async_computation.33 | async-start | bytes 3649536 | tf_op jit(solution)/shard_map/all_gather | solution.py:21
  9.4 237.4 %all-gather.14.cloned.1.call-start = ((), (), s32[]{:S(2)}) async-start(), calls=%async_computation.35 | async-start | bytes 3649536 | tf_op jit(solution)/shard_map/all_gather | solution.py:23
  10.0 301.8 %all-gather.18.cloned.1.call-start = ((), (), s32[]{:S(2)}) async-start(), calls=%async_computation.37 | async-start | bytes 4866048 | tf_op jit(solution)/shard_map/all_gather | solution.py:25
  10.6 365.8 %all-gather.20.cloned.1.call-start = ((), (), s32[]{:S(2)}) async-start(), calls=%async_computation.38 | async-start | bytes 4866048 | tf_op jit(solution)/shard_map/all_gather | solution.py:26
  11.1 453.3 %all-gather.8.cloned.1.call-start = ((), (), s32[]{:S(2)}) async-start(), calls=%async_computation.32 | async-start | bytes 10948608 | tf_op jit(solution)/shard_map/all_gather | solution.py:27
  786.3 21.1 all-to-all-start.4
  807.4 29.5 %all-to-all-start.15 = ((bf16[8,4,18432]{2,0,1:T(8,128)(2,1)}), bf16[8,4,18432]{2,0,1:T(8,128)(2,1)S(1)}, u32[]{:S(2)}, u32[]{:S(2)}) async-start(bf16[8,4,18432]{2,0,1:T(8,128)(2,1)} %copy.291), calls=%async_computation.15 | async-start | bytes 2359296 | tf_op jit(solution)/shard_map/all_to_all | solution.py:77
  836.9 31.6 %all-to-all-start.7 = ((bf16[8,4,18432]{2,0,1:T(8,128)(2,1)}), bf16[8,4,18432]{2,0,1:T(8,128)(2,1)S(1)}, u32[]{:S(2)}, u32[]{:S(2)}) async-start(bf16[8,4,18432]{2,0,1:T(8,128)(2,1)} %copy.283), calls=%async_computation.7 | async-start | bytes 2359296 | tf_op jit(solution)/shard_map/all_to_all | solution.py:59
  868.5 31.6 %all-to-all-start.13 = ((bf16[8,4,18432]{2,0,1:T(8,128)(2,1)}), bf16[8,4,18432]{2,0,1:T(8,128)(2,1)S(1)}, u32[]{:S(2)}, u32[]{:S(2)}) async-start(bf16[8,4,18432]{2,0,1:T(8,128)(2,1)} %copy.289), calls=%async_computation.13 | async-start | bytes 2359296 | tf_op jit(solution)/shard_map/all_to_all | solution.py:77
  900.1 31.6 %all-to-all-start.5 = ((bf16[8,4,18432]{2,0,1:T(8,128)(2,1)}), bf16[8,4,18432]{2,0,1:T(8,128)(2,1)S(1)}, u32[]{:S(2)}, u32[]{:S(2)}) async-start(bf16[8,4,18432]{2,0,1:T(8,128)(2,1)} %copy.282), calls=%async_computation.5 | async-start | bytes 2359296 | tf_op jit(solution)/shard_map/all_to_all | solution.py:59
  932.7 47.1 %all-to-all-start.10 = ((bf16[8,4,55296]{2,1,0:T(4,128)(2,1)}), bf16[8,4,55296]{2,1,0:T(4,128)(2,1)S(1)}, u32[]{:S(2)}, u32[]{:S(2)}) async-start(bf16[8,4,55296]{2,1,0:T(4,128)(2,1)} %convert_element_type.565), calls=%async_computation.10 | async-start | bytes 7077888 | tf_op jit(solution)/shard_map/all_to_all | solution.py:69
  981.6 46.6 %all-to-all-start.8 = ((bf16[8,4,55296]{2,1,0:T(4,128)(2,1)}), bf16[8,4,55296]{2,1,0:T(4,128)(2,1)}, u32[]{:S(2)}, u32[]{:S(2)}) async-start(bf16[8,4,55296]{2,1,0:T(4,128)(2,1)} %convert_element_type.562), calls=%async_computation.8 | async-start | bytes 7077888 | tf_op jit(solution)/shard_map/all_to_all | solution.py:69
  1028.1 45.7 %all-to-all-start.2 = ((bf16[8,4,55296]{2,1,0:T(4,128)(2,1)}), bf16[8,4,55296]{2,1,0:T(4,128)(2,1)S(1)}, u32[]{:S(2)}, u32[]{:S(2)}) async-start(bf16[8,4,55296]{2,1,0:T(4,128)(2,1)} %convert_element_type.553), calls=%async_computation.2 | async-start | bytes 7077888 | tf_op jit(solution)/shard_map/all_to_all | solution.py:51
  1075.6 45.7 %all-to-all-start = ((bf16[8,4,55296]{2,1,0:T(4,128)(2,1)}), bf16[8,4,55296]{2,1,0:T(4,128)(2,1)S(1)}, u32[]{:S(2)}, u32[]{:S(2)}) async-start(bf16[8,4,55296]{2,1,0:T(4,128)(2,1)} %convert_element_type.550), calls=%async_computation | async-start | bytes 7077888 | tf_op jit(solution)/shard_map/all_to_all | solution.py:51
  1123.1 59.3 %all-to-all-start.22 = ((bf16[8,4,73728]{2,1,0:T(4,128)(2,1)}), bf16[8,4,73728]{2,1,0:T(4,128)(2,1)}, u32[]{:S(2)}, u32[]{:S(2)}) async-start(bf16[8,4,73728]{2,1,0:T(4,128)(2,1)} %convert_element_type.585), calls=%async_computation.22 | async-start | bytes 9437184 | tf_op jit(solution)/shard_map/all_to_all | solution.py:96
  1182.4 59.3 %all-to-all-start.18 = ((bf16[8,4,73728]{2,1,0:T(4,128)(2,1)}), bf16[8,4,73728]{2,1,0:T(4,128)(2,1)}, u32[]{:S(2)}, u32[]{:S(2)}) async-start(bf16[8,4,73728]{2,1,0:T(4,128)(2,1)} %convert_element_type.577), calls=%async_computation.18 | async-start | bytes 9437184 | tf_op jit(solution)/shard_map/all_to_all | solution.py:87
  1241.7 59.3 %all-to-all-start.20 = ((bf16[8,4,73728]{2,1,0:T(4,128)(2,1)}), bf16[8,4,73728]{2,1,0:T(4,128)(2,1)}, u32[]{:S(2)}, u32[]{:S(2)}) async-start(bf16[8,4,73728]{2,1,0:T(4,128)(2,1)} %convert_element_type.581), calls=%async_computation.20 | async-start | bytes 9437184 | tf_op jit(solution)/shard_map/all_to_all | solution.py:96
  1301.0 59.4 %all-to-all-start.16 = ((bf16[8,4,73728]{2,1,0:T(4,128)(2,1)}), bf16[8,4,73728]{2,1,0:T(4,128)(2,1)}, u32[]{:S(2)}, u32[]{:S(2)}) async-start(bf16[8,4,73728]{2,1,0:T(4,128)(2,1)} %convert_element_type.574), calls=%async_computation.16 | async-start | bytes 9437184 | tf_op jit(solution)/shard_map/all_to_all | solution.py:87
  1360.4 80.1 %all-to-all-start.11 = ((bf16[8,4,55296]{2,0,1:T(8,128)(2,1)}), bf16[8,4,55296]{2,0,1:T(8,128)(2,1)S(1)}, u32[]{:S(2)}, u32[]{:S(2)}) async-start(bf16[8,4,55296]{2,0,1:T(8,128)(2,1)} %copy.287), calls=%async_computation.11 | async-start | bytes 7077888 | tf_op jit(solution)/shard_map/all_to_all | solution.py:68
  1440.5 83.9 %all-to-all-start.9 = ((bf16[8,4,55296]{2,0,1:T(8,128)(2,1)}), bf16[8,4,55296]{2,0,1:T(8,128)(2,1)}, u32[]{:S(2)}, u32[]{:S(2)}) async-start(bf16[8,4,55296]{2,0,1:T(8,128)(2,1)} %copy.285), calls=%async_computation.9 | async-start | bytes 7077888 | tf_op jit(solution)/shard_map/all_to_all | solution.py:68
  1524.5 83.5 %all-to-all-start.3 = ((bf16[8,4,55296]{2,0,1:T(8,128)(2,1)}), bf16[8,4,55296]{2,0,1:T(8,128)(2,1)}, u32[]{:S(2)}, u32[]{:S(2)}) async-start(bf16[8,4,55296]{2,0,1:T(8,128)(2,1)} %copy.281), calls=%async_computation.3 | async-start | bytes 7077888 | tf_op jit(solution)/shard_map/all_to_all | solution.py:50
  1607.9 83.5 %all-to-all-start.1 = ((bf16[8,4,55296]{2,0,1:T(8,128)(2,1)}), bf16[8,4,55296]{2,0,1:T(8,128)(2,1)}, u32[]{:S(2)}, u32[]{:S(2)}) async-start(bf16[8,4,55296]{2,0,1:T(8,128)(2,1)} %copy.280), calls=%async_computation.1 | async-start | bytes 7077888 | tf_op jit(solution)/shard_map/all_to_all | solution.py:50
  1691.4 123.1 %all-to-all-start.24 = ((bf16[8,4,165888]{2,1,0:T(4,128)(2,1)}), bf16[8,4,165888]{2,1,0:T(4,128)(2,1)}, u32[]{:S(2)}, u32[]{:S(2)}) async-start(bf16[8,4,165888]{2,1,0:T(4,128)(2,1)} %multiply_convert_fusion.1), calls=%async_computation.24 | async-start | bytes 21233664 | tf_op jit(solution)/shard_map/all_to_all | solution.py:105
  1814.4 123.3 %all-to-all-start.26 = ((bf16[8,4,165888]{2,1,0:T(4,128)(2,1)}), bf16[8,4,165888]{2,1,0:T(4,128)(2,1)}, u32[]{:S(2)}, u32[]{:S(2)}) async-start(bf16[8,4,165888]{2,1,0:T(4,128)(2,1)} %multiply_convert_fusion), calls=%async_computation.26 | async-start | bytes 21233664 | tf_op jit(solution)/shard_map/all_to_all | solution.py:105
  1937.7 106.7 %all-to-all-start.23 = ((bf16[8,4,73728]{2,0,1:T(8,128)(2,1)}), bf16[8,4,73728]{2,0,1:T(8,128)(2,1)}, u32[]{:S(2)}, u32[]{:S(2)}) async-start(bf16[8,4,73728]{2,0,1:T(8,128)(2,1)} %copy.295), calls=%async_computation.23 | async-start | bytes 9437184 | tf_op jit(solution)/shard_map/all_to_all | solution.py:95
  2044.5 109.0 %all-to-all-start.19 = ((bf16[8,4,73728]{2,0,1:T(8,128)(2,1)}), bf16[8,4,73728]{2,0,1:T(8,128)(2,1)}, u32[]{:S(2)}, u32[]{:S(2)}) async-start(bf16[8,4,73728]{2,0,1:T(8,128)(2,1)} %copy.293), calls=%async_computation.19 | async-start | bytes 9437184 | tf_op jit(solution)/shard_map/all_to_all | solution.py:86
  2153.4 108.9 %all-to-all-start.21 = ((bf16[8,4,73728]{2,0,1:T(8,128)(2,1)}), bf16[8,4,73728]{2,0,1:T(8,128)(2,1)}, u32[]{:S(2)}, u32[]{:S(2)}) async-start(bf16[8,4,73728]{2,0,1:T(8,128)(2,1)} %copy.294), calls=%async_computation.21 | async-start | bytes 9437184 | tf_op jit(solution)/shard_map/all_to_all | solution.py:95
  2262.4 109.0 %all-to-all-start.17 = ((bf16[8,4,73728]{2,0,1:T(8,128)(2,1)}), bf16[8,4,73728]{2,0,1:T(8,128)(2,1)}, u32[]{:S(2)}, u32[]{:S(2)}) async-start(bf16[8,4,73728]{2,0,1:T(8,128)(2,1)} %copy.292), calls=%async_computation.17 | async-start | bytes 9437184 | tf_op jit(solution)/shard_map/all_to_all | solution.py:86
  2371.4 236.4 %all-to-all-start.25 = ((bf16[8,4,165888]{2,0,1:T(8,128)(2,1)}), bf16[8,4,165888]{2,0,1:T(8,128)(2,1)}, u32[]{:S(2)}, u32[]{:S(2)}) async-start(bf16[8,4,165888]{2,0,1:T(8,128)(2,1)} %copy.296), calls=%async_computation.25 | async-start | bytes 21233664 | tf_op jit(solution)/shard_map/all_to_all | solution.py:104
  2607.7 236.7 %all-to-all-start.27 = ((bf16[8,4,165888]{2,0,1:T(8,128)(2,1)}), bf16[8,4,165888]{2,0,1:T(8,128)(2,1)}, u32[]{:S(2)}, u32[]{:S(2)}) async-start(bf16[8,4,165888]{2,0,1:T(8,128)(2,1)} %copy.297), calls=%async_computation.27 | async-start | bytes 21233664 | tf_op jit(solution)/shard_map/all_to_all | solution.py:104
  (201 other events, 4177.3 us)
Sparse Core Ops, SparseCore 0:
  10.8 56.9 all-gather.11
  70.6 52.9 all-gather.15
  126.3 58.9 all-gather.9
  188.0 58.7 all-gather.13
  249.4 62.3 all-gather.17
  314.5 61.8 all-gather.19
  379.2 85.2 all-gather.7
where the time goes:
time: 2880 us; the launch traced here: 2860 us
  waiting for transfers between devices  2030 us (70%)
  local copies, waits for them, and re-layouts  378 us (13%)
  starting transfers between devices  140 us (5%)
  matrix products  140 us (5%)
  other arithmetic  108 us (4%)
  blocking collectives  42.4 us (1%)
    all_to_all x2, waiting for transfers between devices, spread(): lax.all_to_all(lax.all_to_all(shaped[6].astype(jnp.bfloat16), 'wide', spl...  402 us
    all_to_all x2, waiting for transfers between devices, spread(): lax.all_to_all(shaped[6].astype(jnp.bfloat16), 'wide', split_axis=0, conc...  216 us
    all_to_all x2, waiting for transfers between devices, spread(): lax.all_to_all(lax.all_to_all(shaped[5].astype(jnp.bfloat16), 'wide', spl...  192 us
    all_to_all x2, waiting for transfers between devices, spread(): lax.all_to_all(lax.all_to_all(shaped[4].astype(jnp.bfloat16), 'wide', spl...  189 us
    all_to_all x2, waiting for transfers between devices, spread(): lax.all_to_all(lax.all_to_all(shaped[2].astype(jnp.bfloat16), 'wide', spl...  144 us
    all_to_all x2, waiting for transfers between devices, spread(): lax.all_to_all(shaped[4].astype(jnp.bfloat16), 'wide', split_axis=0, conc...  91.9 us
    all_to_all x2, waiting for transfers between devices, spread(): lax.all_to_all(shaped[5].astype(jnp.bfloat16), 'wide', split_axis=0, conc...  83.3 us
    all_gather x1, waiting for transfers between devices, collect_forward(): lax.all_gather(shards[6], ('wide', 'narrow'), axis=0, tiled=True)  78.8 us
  transfers between devices with their start and end apart: 39, of which 39 were waited for; matrix products, arithmetic and copies ran while one was open for 13% of the time, Pallas kernels for 0%

commit v1 on v0

v1 whole, which is shorter than its diff:
```python
import math

import jax
import jax.numpy as jnp
from jax import lax
from jax.sharding import PartitionSpec as P

D = 768
HEADS = 12
HD = 64
FF = 3072
AXES = ("wide", "narrow")
EPS = 1e-06
MASKED = -1e30
F32 = jnp.float32
BF16 = jnp.bfloat16


def timestep_condition(step_values):
    half_width = D // 2
    frequency = jnp.exp(-math.log(10000.0) * jnp.arange(half_width, dtype=F32) / half_width)
    angles = step_values.astype(F32)[:, None] * frequency
    return jax.nn.silu(jnp.concatenate([jnp.cos(angles), jnp.sin(angles)], axis=-1)).astype(BF16)


def norm_parts(rows):
    centre = rows - jnp.mean(rows, axis=-1, keepdims=True)
    inverse = lax.rsqrt(jnp.mean(centre * centre, axis=-1, keepdims=True) + EPS)
    return centre * inverse, inverse


def norm_back(grad, normed, inverse, scale):
    shift_grad = jnp.sum(grad, axis=1)
    scale_grad = jnp.sum(grad * normed, axis=1)
    pulled = grad * (1.0 + scale)
    back = inverse * (
        pulled
        - jnp.mean(pulled, axis=-1, keepdims=True)
        - normed * jnp.mean(pulled * normed, axis=-1, keepdims=True)
    )
    return back, shift_grad, scale_grad


def dot(a, b):
    return jnp.dot(a, b, preferred_element_type=F32)


def heads(x):
    return x.reshape(x.shape[0], x.shape[1], HEADS, HD)


def attention(low, qkv_w, proj_w, mask):
    packed = dot(low, qkv_w).astype(BF16)
    q, k, v = (heads(part) for part in jnp.split(packed, 3, axis=-1))
    scores = jnp.einsum("bqhd,bkhd->bhqk", q, k, preferred_element_type=F32) * HD ** (-0.5)
    scores = jnp.where(mask, scores, MASKED)
    soft = jax.nn.softmax(scores, axis=-1)
    context = jnp.einsum("bhqk,bkhd->bqhd", soft.astype(BF16), v, preferred_element_type=F32)
    context = context.astype(BF16).reshape(low.shape)
    return dot(context, proj_w), (q, k, v, soft, context)


def attention_back(grad_low, low, qkv_w, proj_w, kept):
    q, k, v, soft, context = kept
    proj_grad = jnp.einsum("bld,ble->de", context, grad_low, preferred_element_type=F32)
    ctx = heads(jnp.einsum("ble,de->bld", grad_low, proj_w, preferred_element_type=F32).astype(BF16))
    v_grad = jnp.einsum("bhqk,bqhd->bkhd", soft.astype(BF16), ctx, preferred_element_type=F32)
    soft_grad = jnp.einsum("bqhd,bkhd->bhqk", ctx, v, preferred_element_type=F32)
    row_dot = jnp.sum(soft_grad * soft, axis=-1, keepdims=True)
    score_grad = (soft * (soft_grad - row_dot)).astype(BF16)
    q_grad = jnp.einsum("bhqk,bkhd->bqhd", score_grad, k, preferred_element_type=F32) * HD ** (-0.5)
    k_grad = jnp.einsum("bhqk,bqhd->bkhd", score_grad, q, preferred_element_type=F32) * HD ** (-0.5)
    packed = jnp.concatenate(
        [part.astype(BF16).reshape(low.shape) for part in (q_grad, k_grad, v_grad)], axis=-1
    )
    qkv_grad = jnp.einsum("bld,ble->de", low, packed, preferred_element_type=F32)
    low_grad = jnp.einsum("ble,de->bld", packed, qkv_w, preferred_element_type=F32)
    return low_grad, qkv_grad, proj_grad


def per_device(latents, buckets, step_ids, qs, ps, qt, pt, up, down, ada, biases, cotangent):
    devices = lax.axis_size(AXES)
    micro = latents.shape[0]
    frames, spatial = latents.shape[2], latents.shape[3]
    tokens = frames * spatial
    rows = D // devices

    steps = lax.all_gather(step_ids[:, 0], AXES, axis=0, tiled=True)
    condition = timestep_condition(steps)
    ada_columns = lax.all_to_all(
        ada.reshape(rows, 9 * D), AXES, split_axis=1, concat_axis=0, tiled=True
    )
    modulation = lax.all_to_all(
        dot(condition, ada_columns), AXES, split_axis=0, concat_axis=1, tiled=True
    )
    bias = lax.all_gather(biases, AXES, axis=0, tiled=True).astype(F32)
    modulation = (modulation + bias[: 9 * D]).reshape(micro, 9, 1, D)
    b_up, b_down = bias[9 * D : 9 * D + FF], bias[9 * D + FF :]

    wide_shard = jnp.concatenate([w.reshape(rows, -1) for w in (qs, ps, qt, pt, up)], axis=1)
    wide = lax.all_gather(wide_shard, AXES, axis=0, tiled=True)
    w_down = lax.all_gather(down.reshape(-1, D), AXES, axis=0, tiled=True)
    cuts = [3 * D, 4 * D, 7 * D, 8 * D]
    w_qs, w_ps, w_qt, w_pt, w_up = jnp.split(wide, cuts, axis=1)

    positions = jnp.arange(tokens)
    frame, place = positions // spatial, positions % spatial
    bucket = buckets[:, 0]
    length = jnp.where(bucket == 0, spatial, jnp.where(bucket == 1, spatial // 2, spatial // 8))
    valid = place[None, :] < length[:, None]
    space_mask = (frame[:, None] == frame[None, :])[None, None] & valid[:, None, None, :]
    time_mask = (place[:, None] == place[None, :])[None, None]
    valid_rows = valid.astype(F32)[:, :, None]

    sh1, sc1, ga1, sh2, sc2, ga2, sh3, sc3, ga3 = (modulation[:, i] for i in range(9))
    x = latents.reshape(micro, tokens, D).astype(F32)
    n1, r1 = norm_parts(x)
    h1 = (n1 * (1.0 + sc1) + sh1).astype(BF16)
    a1, kept1 = attention(h1, w_qs, w_ps, space_mask)
    x1 = x + ga1 * a1
    n2, r2 = norm_parts(x1)
    h2 = (n2 * (1.0 + sc2) + sh2).astype(BF16)
    a2, kept2 = attention(h2, w_qt, w_pt, time_mask)
    x2 = x1 + ga2 * a2
    n3, r3 = norm_parts(x2)
    h3 = (n3 * (1.0 + sc3) + sh3).astype(BF16)
    hidden = dot(h3, w_up) + b_up
    gelu, pull = jax.vjp(lambda u: jax.nn.gelu(u, approximate=True), hidden)
    g = gelu.astype(BF16)
    m = dot(g, w_down) + b_down
    x3 = x2 + ga3 * m
    output = (x3 * valid_rows).astype(BF16)

    d3 = cotangent.reshape(micro, tokens, D).astype(F32) * valid_rows
    dm = (ga3 * d3).astype(BF16)
    dga3 = jnp.sum(d3 * m, axis=1)
    db_down = jnp.sum(dm.astype(F32), axis=(0, 1))
    dw_down = jnp.einsum("bsk,bsd->kd", g, dm, preferred_element_type=F32)
    dg = jnp.einsum("bsd,kd->bsk", dm, w_down, preferred_element_type=F32)
    du = pull(dg)[0].astype(BF16)
    db_up = jnp.sum(du.astype(F32), axis=(0, 1))
    dw_up = jnp.einsum("bsd,bsk->dk", h3, du, preferred_element_type=F32)
    dh3 = jnp.einsum("bsk,dk->bsd", du, w_up, preferred_element_type=F32)
    dv, dsh3, dsc3 = norm_back(dh3, n3, r3, sc3)
    d2 = d3 + dv
    da2 = (ga2 * d2).astype(BF16)
    dga2 = jnp.sum(d2 * a2, axis=1)
    dh2, dw_qt, dw_pt = attention_back(da2, h2, w_qt, w_pt, kept2)
    dv, dsh2, dsc2 = norm_back(dh2, n2, r2, sc2)
    d1 = d2 + dv
    da1 = (ga1 * d1).astype(BF16)
    dga1 = jnp.sum(d1 * a1, axis=1)
    dh1, dw_qs, dw_ps = attention_back(da1, h1, w_qs, w_ps, kept1)
    dv, dsh1, dsc1 = norm_back(dh1, n1, r1, sc1)
    latents_grad = d1 + dv

    dmod = jnp.concatenate([dsh1, dsc1, dga1, dsh2, dsc2, dga2, dsh3, dsc3, dga3], axis=-1)
    small = jnp.concatenate([dmod.reshape(1, -1), db_up[None], db_down[None]], axis=-1)
    small = lax.all_gather(small.astype(BF16), AXES, axis=0, tiled=True)
    dmod_all = small[:, : micro * 9 * D].reshape(devices * micro, 9 * D)
    me = lax.axis_index(AXES)
    my_condition = lax.dynamic_slice_in_dim(condition, me * rows, rows, axis=1)
    dw_ada = lax.dot_general(
        my_condition, dmod_all, (((0,), (0,)), ((), ())), preferred_element_type=F32
    )
    db = jnp.concatenate(
        [
            jnp.sum(dmod_all.astype(F32), axis=0),
            jnp.sum(small[:, micro * 9 * D :].astype(F32), axis=0),
        ]
    )
    db = lax.dynamic_slice_in_dim(db, me * biases.shape[0], biases.shape[0])

    dwide = jnp.concatenate([w.astype(BF16) for w in (dw_qs, dw_ps, dw_qt, dw_pt, dw_up)], axis=1)
    dwide = lax.psum_scatter(dwide, AXES, scatter_dimension=0, tiled=True).astype(F32)
    ddown = lax.psum_scatter(dw_down.astype(BF16), AXES, scatter_dimension=0, tiled=True).astype(F32)
    flat = tuple(part.reshape(-1) for part in jnp.split(dwide, cuts, axis=1))
    shape = latents.shape
    return (
        output.reshape(shape),
        latents_grad.reshape(shape),
        *flat,
        ddown.reshape(-1),
        dw_ada.reshape(-1),
        db,
    )


def solution(mesh):
    items = P(None, AXES, None, None, None)
    flat = P(AXES)
    return jax.shard_map(
        per_device,
        mesh=mesh,
        in_specs=(items, P(None, AXES), P(None, AXES)) + (flat,) * 8 + (items,),
        out_specs=(items, items) + (flat,) * 8,
        check_vma=False,
    )
```

time: 2880 us -> 645 us (0.22)
  waiting for transfers between devices: 2030 us -> 302 us
  local copies, waits for them, and re-layouts: 378 us -> 62.7 us
  starting transfers between devices: 140 us -> 11.9 us
  other arithmetic: 108 us -> 18.9 us
  blocking collectives: 42.4 us -> 86.5 us
    all_to_all x32 -> x2, waiting for transfers between devices: 1670 us -> 0.01 us  [the longest x1 0.01 us: per_device(): lax.all_to_all(dot(condition, ada_columns), AXES, split_axis=0, concat_ax...]
    all_gather x7 -> x3, waiting for transfers between devices: 360 us -> 29.1 us  [the longest x1 12.8 us: per_device(): small = lax.all_gather(small.astype(BF16), AXES, axis=0, tiled=True)]
    reduce_scatter x0 -> x2, waiting for transfers between devices: none -> 273 us  [the longest x1 166 us: per_device(): lax.psum_scatter(dwide, AXES, scatter_dimension=0, tiled=True).astype(F32)]
    all_to_all x32 -> x2, starting transfers between devices: 140 us -> 11.7 us  [the longest x1 7.33 us: per_device(): lax.all_to_all(ada.reshape(rows, 9 * D), AXES, split_axis=1, concat_axis=...]
    convert_element_type x26 -> x4, local copies, waits for them, and re-layouts: 93.7 us -> 8.8 us  [the longest x2 4.61 us: attention_back(): jnp.einsum('ble,de->bld', grad_low, proj_w, preferred_element_type=F32)]
    all_to_all x16 -> x4, local copies, waits for them, and re-layouts: 83.4 us -> 2.33 us  [the longest x2 2.22 us: per_device(): lax.all_to_all(ada.reshape(rows, 9 * D), AXES, split_axis=1, concat_axis=...]
    reshape x19, local copies, waits for them, and re-layouts: 92.5 us -> 24.1 us  [the longest x6 12.8 us: attention_back(): part.astype(BF16).reshape(low.shape)]
    mul x8 -> x2, local copies, waits for them, and re-layouts: 65.4 us -> 0.17 us  [timestep_condition(): angles = step_values.astype(F32)[:, None] * frequency]
  transfers between devices with their start and end apart: 39 -> 7, of which waited for: 39 -> 5; matrix products, arithmetic and copies ran while one was open for 13% -> 17% of each run, Pallas kernels for 0% -> 0%
where the time goes in v1:
time: 645 us; the launch traced here: 639 us
  waiting for transfers between devices  302 us (47%)
  matrix products  141 us (22%)
  blocking collectives  86.5 us (13%)
  local copies, waits for them, and re-layouts  62.7 us (10%)
  other arithmetic  18.9 us (3%)
  between operations  15.5 us (2%)
  starting transfers between devices  11.9 us (2%)
    reduce_scatter x1, waiting for transfers between devices, per_device(): lax.psum_scatter(dwide, AXES, scatter_dimension=0, tiled=True).astype(F32)  166 us
    reduce_scatter x1, waiting for transfers between devices, per_device(): lax.psum_scatter(dw_down.astype(BF16), AXES, scatter_dimension=0, tiled=T...  107 us
    unnamed x2, blocking collectives  86.5 us
    dot_general x7, matrix products, dot(): return jnp.dot(a, b, preferred_element_type=F32)  28 us
    dot_general x2, matrix products, attention_back(): jnp.einsum('bqhd,bkhd->bhqk', ctx, v, preferred_element_type=F32)  13.4 us
  transfers between devices with their start and end apart: 7, of which 5 were waited for; matrix products, arithmetic and copies ran while one was open for 17% of the time, Pallas kernels for 0%

profile of v1, /device:TPU:0, one launch (start us, length us, event | category | flops | bytes accessed | tf_op | source)
XLA Modules:
  0.0 638.9 jit_solution(3577207136984138189)
XLA Ops:
  15.2 7.3 %all-to-all-start = ((bf16[24,32,216]{2,0,1:T(8,128)(2,1)}), bf16[24,32,216]{2,0,1:T(8,128)(2,1)S(1)}, u32[]{:S(2)}, u32[]{:S(2)}) async-start(bf16[24,32,216]{2,0,1:T(8,128)(2,1)} %copy.107), calls=%async_computation | async-start | bytes 786432 | tf_op jit(solution)/shard_map/all_to_all | solution.py:90
  23.7 42.4 %all-reduce = s32[64]{0:T(128)S(1)} all-reduce(s32[64]{0:T(128)S(1)} %bitcast_dynamic-update-slice_fusion), channel_id=2, replica_groups=mesh['wide'=8,'narrow'=4] {'wide','narrow'}, use_global_device_ids=true, to_apply=%add | all-reduce | flops 64 | bytes 512
  68.6 4.4 all-to-all-start.1
  73.5 44.1 %all-reduce.1 = bf16[10752]{0:T(1024)(128)(2,1)S(1)} all-reduce(bf16[10752]{0:T(1024)(128)(2,1)S(1)} %dynamic-update-slice.1), channel_id=1, replica_groups=mesh['wide'=8,'narrow'=4] {'wide','narrow'}, use_global_device_ids=true, to_apply=%add.1 | all-reduce | flops 10752 | bytes 43008
  119.9 5.7 all-gather.6.cloned.1.call-done
  125.6 4.0 convolution_convert_fusion.1
  133.5 4.8 fusion.104
  141.7 3.6 fusion.98
  145.6 4.1 convolution_convert_fusion
  158.1 6.5 %fusion.105 = (f32[2,12,256]{2,1,0:T(8,128)S(1)}, f32[2,12,256,256]{2,3,1,0:T(8,128)}) fusion(pred[256,256]{0,1:T(8,128)(4,1)S(1)} %broadcast_compare_fusion, bf16[2,256,12,64]{1,3,2,0:T(8,128)(2,1)} %bitcast.222, bf16[2,256,12,64]{1,3,2,0:T(8,128)(2,1)} %bitcast.220), kind=kOutput, calls=%fused_computation.229 | convolution fusion | flops 207618304 | bytes 7954432 | tf_op jit(solution)/shard_map/sub | solution.py:57
  164.6 3.7 fusion.58
  168.3 3.5 fusion.97
  173.1 7.0 %fusion.19 = f32[2,256,3072]{2,1,0:T(8,128)} fusion(bf16[768,9216]{1,0:T(8,128)(2,1)} %all-gather.6.cloned.1.call-done, f32[2,256,768]{2,1,0:T(8,128)S(1)} %get-tuple-element.59, f32[2,768]{1,0:T(2,128)S(1)} %get-tuple-element.104, f32[2,768]{1,0:T(2,128)S(1)} %get-tuple-element.105, f32[2,256]{1,0:T(2,128)S(1)} %add_rsqrt_fusion.1, ...), kind=kOutput, calls=%fused_computation.37 | convolution fusion | flops 2417885184 | bytes 12599296 | tf_op jit(solution)/shard_map/dot_general | solution.py:45
  180.1 10.6 %all-gather.8.cloned.1.call-done = bf16[3072,768]{1,0:T(8,128)(2,1)} async-done(((bf16[96,768]{1,0:T(8,128)(2,1)}), bf16[3072,768]{1,0:T(8,128)(2,1)}) %all-gather.8.cloned.1.call-update) | async-done | bytes 4718608 | tf_op jit(solution)/shard_map/all_gather | solution.py:102
  190.7 9.2 %fusion.106 = (bf16[3072]{0:T(1024)(128)(2,1)S(1)}, bf16[2,256,3072]{2,1,0:T(8,128)(2,1)S(1)}) fusion(f32[2,256,3072]{2,1,0:T(8,128)} %fusion.19, f32[3072]{0:T(1024)S(1)} %slice.75, bf16[2,256,768]{2,1,0:T(8,128)(2,1)} %multiply_convert_fusion.10, bf16[3072,768]{1,0:T(8,128)(2,1)} %all-gather.8.cloned.1.call-done), kind=kOutput, calls=%fused_computation.230 | convolution fusion | flops 2450519040 | bytes 14960640 | tf_op jit(solution)/shard_map/bsd,kd->bsk/dot_general | solution.py:139
  200.0 6.6 %multiply_reduce_fusion.3 = (bf16[2,768]{1,0:T(2,128)(2,1)S(1)}, f32[2,256]{1,0:T(2,128)S(1)}, f32[2,256]{1,0:T(2,128)S(1)}, bf16[2,768]{1,0:T(2,128)(2,1)S(1)}, f32[2,256,768]{2,1,0:T(8,128)S(1)}) fusion(f32[2,256,768]{2,1,0:T(8,128)S(1)} %copy-done.4, f32[2,256]{1,0:T(2,128)S(1)} %add_rsqrt_fusion.1, f32[2,256]{1,0:T(2,128)S(1)} %broadcast_multiply_fusion.7, ...), kind=kOutput, calls=%fused_computation.76 | convolution fusion | flops 2419453952 | bytes 11030528 | tf_op jit(solution)/shard_map/bsk,dk->bsd/dot_general | solution.py:143
  207.3 5.5 multiply_reduce_fusion.2
  219.3 5.1 fusion.61
  224.5 6.7 %multiply_reduce_fusion.1 = (f32[2,12,256]{2,1,0:T(8,128)S(1)}, f32[2,12,256,256]{2,3,1,0:T(8,128)}) fusion(f32[2,12,256,256]{2,3,1,0:T(8,128)} %get-tuple-element.93, f32[2,12,256]{2,1,0:T(8,128)S(1)} %get-tuple-element.92, bf16[2,256,12,64]{1,3,2,0:T(8,128)(2,1)S(1)} %bitcast.240, bf16[2,256,12,64]{1,3,2,0:T(8,128)(2,1)S(1)} %bitcast.236), kind=kOutput, calls=%fused_computation.18 | convolution fusion | flops 206039040 | bytes 14204928 | tf_op jit(solution)/shard_map/bqhd,bkhd->bhqk/dot_general | solution.py:68
  231.2 4.3 multiply_convert_fusion.1
  246.0 5.3 multiply_reduce_fusion.5
  258.5 5.1 fusion.55
  263.7 6.7 %multiply_reduce_fusion = (f32[2,12,256]{2,1,0:T(8,128)S(1)}, f32[2,12,256,256]{2,3,1,0:T(8,128)}) fusion(f32[2,12,256,256]{2,3,1,0:T(8,128)} %get-tuple-element.90, f32[2,12,256]{2,1,0:T(8,128)S(1)} %get-tuple-element.89, bf16[2,256,12,64]{1,3,2,0:T(8,128)(2,1)S(1)} %bitcast.242, bf16[2,256,12,64]{1,3,2,0:T(8,128)(2,1)S(1)} %bitcast.234), kind=kOutput, calls=%fused_computation.16 | convolution fusion | flops 206039040 | bytes 14204928 | tf_op jit(solution)/shard_map/bqhd,bkhd->bhqk/dot_general | solution.py:68
  270.3 4.5 multiply_convert_fusion
  284.3 6.8 %fusion.43 = (bf16[2,768]{1,0:T(2,128)(2,1)S(1)}, f32[2,256]{1,0:T(2,128)}, f32[2,256]{1,0:T(2,128)}, bf16[2,768]{1,0:T(2,128)(2,1)S(1)}, f32[2,256,768]{2,1,0:T(8,128)}) fusion(bf16[2,1,16,16,768]{4,3,2,1,0:T(8,128)(2,1)S(1)} %copy-done, f32[2,256]{1,0:T(2,128)S(1)} %rsqrt.28, f32[2,256]{1,0:T(2,128)S(1)} %div.81, f32[2,768]{1,0:T(2,128)S(1)} %get-tuple-element.110, ...), kind=kOutput, calls=%fused_computation.73 | convolution fusion | flops 1822945280 | bytes 8278016 | tf_op jit(solution)/shard_map/ble,de->bld/dot_general | solution.py:77
  292.1 8.6 %bitcast_convert_fusion = bf16[3072,768]{1,0:T(8,128)(2,1)} fusion(bf16[2,256,768]{2,1,0:T(8,128)(2,1)S(1)} %copy-done.23, f32[2,256,3072]{2,1,0:T(8,128)} %fusion.19, f32[3072]{0:T(1024)S(1)} %slice.75), kind=kOutput, calls=%fused_computation.2 | convolution fusion | flops 2434007040 | bytes 11808768 | tf_op jit(solution)/shard_map/bsk,bsd->kd/dot_general | solution.py:138
  312.8 5.8 fusion.10
  319.9 4.1 fusion.11
  325.2 4.8 fusion.9
  334.6 12.8 %all-gather.10.cloned.1.call-done = bf16[32,1,17664]{2,1,0:T(2,128)(2,1)} async-done(((bf16[1,1,17664]{2,1,0:T(2,128)(2,1)}), bf16[32,1,17664]{2,1,0:T(2,128)(2,1)}) %all-gather.10.cloned.1.call-update) | async-done | bytes 1130512 | tf_op jit(solution)/shard_map/all_gather | solution.py:159
  351.8 107.3 %reduce-scatter.5.cloned.1.call-done = bf16[96,768]{1,0:T(8,128)(2,1)} async-done(((bf16[3072,768]{1,0:T(8,128)(2,1)}), bf16[96,768]{1,0:T(8,128)(2,1)}) %reduce-scatter.5.cloned.1.call-update) | async-done | bytes 147472 | tf_op jit(solution)/shard_map/reduce_scatter | solution.py:176
  460.9 165.7 %reduce-scatter.3.cloned.1.call-done = bf16[24,9216]{1,0:T(8,128)(2,1)} async-done(((bf16[768,9216]{1,0:T(8,128)(2,1)}), bf16[24,9216]{1,0:T(8,128)(2,1)}) %reduce-scatter.3.cloned.1.call-update) | async-done | bytes 442384 | tf_op jit(solution)/shard_map/reduce_scatter | solution.py:175
  (288 shorter events, 96.8 us)
Async XLA Ops:
  7.2 15.4 %copy-start.34 = (bf16[73728]{0:T(1024)(128)(2,1)S(1)}, bf16[73728]{0:T(1024)(128)(2,1)}, u32[]{:S(2)}) copy-start(bf16[73728]{0:T(1024)(128)(2,1)} %param.20) | copy-start | bytes 442372
  7.2 118.4 %all-gather.6.cloned.1.call-start = ((), (), s32[]{:S(2)}) async-start(), calls=%async_computation.4 | async-start | bytes 14598144 | tf_op jit(solution)/shard_map/all_gather | solution.py:101
  10.0 13.6 %copy-start.63 = (s32[2,1]{0,1:T(1,128)S(1)}, s32[2,1]{0,1:T(1,128)}, u32[]{:S(2)}) copy-start(s32[2,1]{0,1:T(1,128)} %param.13) | copy-start | bytes 28
  10.0 13.6 %copy-start.64 = (s32[2,1]{0,1:T(1,128)S(1)}, s32[2,1]{0,1:T(1,128)}, u32[]{:S(2)}) copy-start(s32[2,1]{0,1:T(1,128)} %param.14) | copy-start | bytes 28
  10.0 56.3 %copy-start = (bf16[2,1,16,16,768]{4,3,2,1,0:T(8,128)(2,1)S(1)}, bf16[2,1,16,16,768]{4,3,2,1,0:T(8,128)(2,1)}, u32[]{:S(2)}) copy-start(bf16[2,1,16,16,768]{4,3,2,1,0:T(8,128)(2,1)} %param.12) | copy-start | bytes 2359300
  15.2 52.5 %all-to-all-start = ((bf16[24,32,216]{2,0,1:T(8,128)(2,1)}), bf16[24,32,216]{2,0,1:T(8,128)(2,1)S(1)}, u32[]{:S(2)}, u32[]{:S(2)}) async-start(bf16[24,32,216]{2,0,1:T(8,128)(2,1)} %copy.107), calls=%async_computation | async-start | bytes 786432 | tf_op jit(solution)/shard_map/all_to_all | solution.py:90
  22.6 50.6 %copy-start.61 = (bf16[336]{0:T(512)(128)(2,1)S(1)}, bf16[336]{0:T(512)(128)(2,1)}, u32[]{:S(2)}) copy-start(bf16[336]{0:T(512)(128)(2,1)} %param.22) | copy-start | bytes 2020
  22.6 168.1 %all-gather.8.cloned.1.call-start = ((), (), s32[]{:S(2)}) async-start(), calls=%async_computation.5 | async-start | bytes 4866048 | tf_op jit(solution)/shard_map/all_gather | solution.py:102
  23.5 94.4 %copy-start.41 = (f32[384]{0:T(512)}, f32[384]{0:T(512)S(1)}, u32[]{:S(2)}) copy-start(f32[384]{0:T(512)S(1)} %multiply_exponential_fusion) | copy-start | bytes 4612
  66.1 51.8 %copy-start.55 = (f32[64]{0:T(128)}, f32[64]{0:T(128)S(1)}, u32[]{:S(2)}) copy-start(f32[64]{0:T(128)S(1)} %convert_element_type.249) | copy-start | bytes 772
  66.3 51.7 %copy-start.15 = (bf16[2,1,16,16,768]{4,3,2,1,0:T(8,128)(2,1)S(1)}, bf16[2,1,16,16,768]{4,3,2,1,0:T(8,128)(2,1)}, u32[]{:S(2)}) copy-start(bf16[2,1,16,16,768]{4,3,2,1,0:T(8,128)(2,1)} %param.23) | copy-start | bytes 2359300
  68.6 49.1 %all-to-all-start.1 = ((f32[32,2,216]{2,1,0:T(2,128)}), f32[32,2,216]{2,1,0:T(2,128)S(1)}, u32[]{:S(2)}, u32[]{:S(2)}) async-start(f32[32,2,216]{2,1,0:T(2,128)} %copy.109), calls=%async_computation.1 | async-start | bytes 131072 | tf_op jit(solution)/shard_map/all_to_all | solution.py:93
  73.0 274.5 %all-gather.10.cloned.1.call-start = ((), (), s32[]{:S(2)}) async-start(), calls=%async_computation.8 | async-start | bytes 2331648 | tf_op jit(solution)/shard_map/all_gather | solution.py:159
  73.2 211.1 %copy-start.37 = (f32[2,256]{1,0:T(2,128)}, f32[2,256]{1,0:T(2,128)S(1)}, u32[]{:S(2)}) copy-start(f32[2,256]{1,0:T(2,128)S(1)} %div.81) | copy-start | bytes 6148
  117.7 166.6 %copy-start.39 = (f32[2,256]{1,0:T(2,128)}, f32[2,256]{1,0:T(2,128)S(1)}, u32[]{:S(2)}) copy-start(f32[2,256]{1,0:T(2,128)S(1)} %rsqrt.28) | copy-start | bytes 6148
  117.9 133.4 %copy-start.35 = (f32[2,768]{1,0:T(2,128)}, f32[2,768]{1,0:T(2,128)S(1)}, u32[]{:S(2)}) copy-start(f32[2,768]{1,0:T(2,128)S(1)} %get-tuple-element.107) | copy-start | bytes 18436
  118.3 53.9 %copy-start.49 = (f32[2,768]{1,0:T(2,128)}, f32[2,768]{1,0:T(2,128)S(1)}, u32[]{:S(2)}) copy-start(f32[2,768]{1,0:T(2,128)S(1)} %get-tuple-element.104) | copy-start | bytes 18436
  118.3 88.3 %copy-start.51 = (f32[2,768]{1,0:T(2,128)}, f32[2,768]{1,0:T(2,128)S(1)}, u32[]{:S(2)}) copy-start(f32[2,768]{1,0:T(2,128)S(1)} %get-tuple-element.105) | copy-start | bytes 18436
  118.3 27.2 %copy-start.53 = (f32[2,768]{1,0:T(2,128)}, f32[2,768]{1,0:T(2,128)S(1)}, u32[]{:S(2)}) copy-start(f32[2,768]{1,0:T(2,128)S(1)} %get-tuple-element.108) | copy-start | bytes 18436
  145.2 106.1 %copy-start.43 = (f32[2,256]{1,0:T(2,128)}, f32[2,256]{1,0:T(2,128)S(1)}, u32[]{:S(2)}) copy-start(f32[2,256]{1,0:T(2,128)S(1)} %broadcast_multiply_fusion.8) | copy-start | bytes 6148
  145.6 105.8 %copy-start.47 = (f32[2,256]{1,0:T(2,128)}, f32[2,256]{1,0:T(2,128)S(1)}, u32[]{:S(2)}) copy-start(f32[2,256]{1,0:T(2,128)S(1)} %add_rsqrt_fusion.2) | copy-start | bytes 6148
  171.9 34.7 %copy-start.45 = (f32[2,256]{1,0:T(2,128)}, f32[2,256]{1,0:T(2,128)S(1)}, u32[]{:S(2)}) copy-start(f32[2,256]{1,0:T(2,128)S(1)} %broadcast_multiply_fusion.7) | copy-start | bytes 6148
  172.2 34.4 %copy-start.57 = (f32[2,256]{1,0:T(2,128)}, f32[2,256]{1,0:T(2,128)S(1)}, u32[]{:S(2)}) copy-start(f32[2,256]{1,0:T(2,128)S(1)} %add_rsqrt_fusion.1) | copy-start | bytes 6148
  190.7 9.2 %copy-start.4 = (f32[2,256,768]{2,1,0:T(8,128)S(1)}, f32[2,256,768]{2,1,0:T(8,128)}, u32[]{:S(2)}) copy-start(f32[2,256,768]{2,1,0:T(8,128)} %copy-done.3) | copy-start | bytes 4718596
  200.0 7.4 %copy-start.65 = (f32[2,256,3072]{2,1,0:T(8,128)S(1)}, f32[2,256,3072]{2,1,0:T(8,128)}, u32[]{:S(2)}) copy-start(f32[2,256,3072]{2,1,0:T(8,128)} %fusion.19) | copy-start | bytes 18874372
  219.3 11.8 %slice-start.2 = ((s8[6291456]{0:T(1024)(128)(4,1)}), s8[4194304]{0:T(1024)(128)(4,1)S(1)}, s32[]{:S(2)}) async-start(s8[6291456]{0:T(1024)(128)(4,1)} %bitcast.212), calls=%async_computation.11 | async-start | bytes 8388608
  258.5 11.8 %slice-start = ((s8[6291456]{0:T(1024)(128)(4,1)}), s8[4194304]{0:T(1024)(128)(4,1)S(1)}, s32[]{:S(2)}) async-start(s8[6291456]{0:T(1024)(128)(4,1)} %bitcast.210), calls=%async_computation.9 | async-start | bytes 8388608
  284.3 7.7 %copy-start.23 = (bf16[2,256,768]{2,1,0:T(8,128)(2,1)S(1)}, bf16[2,256,768]{2,1,0:T(8,128)(2,1)}, u32[]{:S(2)}) copy-start(bf16[2,256,768]{2,1,0:T(8,128)(2,1)} %multiply_convert_fusion.10) | copy-start | bytes 2359300
  292.0 167.2 %reduce-scatter.5.cloned.1.call-start = ((), (), s32[]{:S(2)}) async-start(), calls=%async_computation.7 | async-start | bytes 4866048 | tf_op jit(solution)/shard_map/reduce_scatter | solution.py:176
  300.6 325.9 %reduce-scatter.3.cloned.1.call-start = ((), (), s32[]{:S(2)}) async-start(), calls=%async_computation.6 | async-start | bytes 14598144 | tf_op jit(solution)/shard_map/reduce_scatter | solution.py:175
  312.7 7.1 %copy-start.25 = (bf16[2,256,768]{2,1,0:T(8,128)(2,1)S(1)}, bf16[2,256,768]{2,1,0:T(8,128)(2,1)}, u32[]{:S(2)}) copy-start(bf16[2,256,768]{2,1,0:T(8,128)(2,1)} %copy.125) | copy-start | bytes 2359300
  312.7 7.1 %copy-start.26 = (bf16[2,256,768]{2,1,0:T(8,128)(2,1)S(1)}, bf16[2,256,768]{2,1,0:T(8,128)(2,1)}, u32[]{:S(2)}) copy-start(bf16[2,256,768]{2,1,0:T(8,128)(2,1)} %copy.126) | copy-start | bytes 2359300
  (47 other events, 206.6 us)
Sparse Core Ops, SparseCore 0:
  13.1 112.3 all-gather.5
  128.9 61.7 all-gather.7
  292.1 55.2 all-gather.9
  352.8 106.3 reduce-scatter.4
  465.0 161.5 reduce-scatter.2

commit v2 on v1

--- a/solution.py
+++ b/solution.py
@@ -3,6 +3,8 @@
 import jax
 import jax.numpy as jnp
 from jax import lax
+from jax.experimental import pallas as pl
+from jax.experimental.pallas import tpu as pltpu
 from jax.sharding import PartitionSpec as P
 
 D = 768
@@ -77,6 +79,338 @@
     low_grad = jnp.einsum("ble,de->bld", packed, qkv_w, preferred_element_type=F32)
     return low_grad, qkv_grad, proj_grad
 
+MESH = pl.DeviceIdType.MESH
+
+
+def place():
+    w, z = lax.axis_index("wide"), lax.axis_index("narrow")
+    return w // 4, (w // 2) % 2, w % 2, z
+
+
+def device_at(y, x, c, z):
+    return {"wide": (y * 2 + x) * 2 + c, "narrow": z}
+
+
+def greet(here):
+    y, x, c, z = here
+    barrier = pltpu.get_barrier_semaphore()
+    partners = [device_at(y, x, 1 - c, z), device_at(y, 1 - x, c, z), device_at(1 - y, x, c, z)]
+    partners += [device_at(y, x, c, (z + step) % 4) for step in (1, 2, 3)]
+    for partner in partners:
+        pl.semaphore_signal(barrier, inc=1, device_id=partner, device_id_type=MESH)
+    pl.semaphore_wait(barrier, 6)
+
+
+def remote(src, dst, send, recv, target):
+    return pltpu.make_async_remote_copy(
+        src_ref=src, dst_ref=dst, send_sem=send, recv_sem=recv,
+        device_id=target, device_id_type=MESH,
+    )
+
+
+class Sender:
+    def __init__(self):
+        self.copies = []
+
+    def go(self, src, dst, send, recv, target):
+        copy = remote(src, dst, send, recv, target)
+        copy.start()
+        self.copies.append(copy)
+
+    def drain(self):
+        for copy in self.copies:
+            copy.wait_send()
+
+
+class Gather:
+    SEMAPHORES = (3, 3, 10, 10, 3, 3, 3, 3)
+
+    def __init__(self, here, sender, own, out, semaphores, local):
+        self.here, self.sender, self.own, self.out, self.local = here, sender, own, out, local
+        self.zs, self.zr, self.cs, self.cr, self.xs, self.xr, self.ys, self.yr = semaphores
+        y, x, c, z = here
+        self.sib = device_at(y, x, 1 - c, z)
+        self.xn = device_at(y, 1 - x, c, z)
+        self.yn = device_at(1 - y, x, c, z)
+
+    @staticmethod
+    def scratch(count):
+        kinds = [pltpu.SemaphoreType.DMA((count, k)) for k in Gather.SEMAPHORES]
+        return kinds + [pltpu.SemaphoreType.DMA((count,))]
+
+    def start(self):
+        y, x, c, z = self.here
+        count = len(self.own)
+        for i in range(count):
+            for step in (2, 1, 3):
+                self.sender.go(
+                    self.own[i], self.out[i].at[y, x, c, z], self.zs.at[i, step - 1],
+                    self.zr.at[i, step - 1], device_at(y, x, c, (z + step) % 4),
+                )
+        for i in range(count):
+            mine = self.out[i].at[y, x, c, z]
+            pltpu.make_async_copy(self.own[i], mine, self.local.at[i]).start()
+            self.sender.go(self.own[i], mine, self.cs.at[i, 0], self.cr.at[i, 0], self.sib)
+
+    def along(self, ref, send, recv, target):
+        self.sender.go(ref, ref, send, recv, target)
+
+    def arrived(self, ref, send, recv):
+        remote(ref, ref, send, recv, self.sib).wait_recv()
+
+    def across(self, i, k, ref):
+        self.sender.go(ref, ref, self.cs.at[i, k], self.cr.at[i, k], self.sib)
+
+    def stage1(self, i):
+        y, x, c, z = self.here
+        out = self.out[i]
+        pltpu.make_async_copy(self.own[i], out.at[y, x, c, z], self.local.at[i]).wait()
+        for step in (1, 2, 3):
+            self.arrived(out.at[y, x, c, (z + 4 - step) % 4], self.zs.at[i, step - 1], self.zr.at[i, step - 1])
+        low, high = out.at[y, x, c, pl.ds(0, 2)], out.at[y, x, c, pl.ds(2, 2)]
+        self.along(low, self.xs.at[i, 0], self.xr.at[i, 0], self.xn)
+        self.along(high, self.ys.at[i, 0], self.yr.at[i, 0], self.yn)
+        self.along(high, self.xs.at[i, 1], self.xr.at[i, 1], self.xn)
+        self.along(low, self.ys.at[i, 1], self.yr.at[i, 1], self.yn)
+        for step in (1, 2, 3):
+            self.across(i, step, out.at[y, x, c, (z + 4 - step) % 4])
+
+    def stage2(self, i):
+        y, x, c, z = self.here
+        low_x = self.out[i].at[y, 1 - x, c, pl.ds(0, 2)]
+        high_y = self.out[i].at[1 - y, x, c, pl.ds(2, 2)]
+        self.arrived(low_x, self.xs.at[i, 0], self.xr.at[i, 0])
+        self.along(low_x, self.ys.at[i, 2], self.yr.at[i, 2], self.yn)
+        self.arrived(high_y, self.ys.at[i, 0], self.yr.at[i, 0])
+        self.along(high_y, self.xs.at[i, 2], self.xr.at[i, 2], self.xn)
+        self.across(i, 4, low_x)
+        self.across(i, 5, high_y)
+
+    def stage3(self, i):
+        y, x, c, z = self.here
+        out = self.out[i]
+        arrivals = (
+            (out.at[y, 1 - x, c, pl.ds(2, 2)], self.xs.at[i, 1], self.xr.at[i, 1]),
+            (out.at[1 - y, x, c, pl.ds(0, 2)], self.ys.at[i, 1], self.yr.at[i, 1]),
+            (out.at[1 - y, 1 - x, c, pl.ds(2, 2)], self.xs.at[i, 2], self.xr.at[i, 2]),
+            (out.at[1 - y, 1 - x, c, pl.ds(0, 2)], self.ys.at[i, 2], self.yr.at[i, 2]),
+        )
+        for k, (ref, send, recv) in enumerate(arrivals):
+            self.arrived(ref, send, recv)
+            self.across(i, 6 + k, ref)
+
+    def finish(self, i):
+        y, x, c, z = self.here
+        o = 1 - c
+        out = self.out[i]
+        arrivals = [out.at[y, x, o, (z + 4 - step) % 4] for step in (0, 1, 2, 3)]
+        arrivals += [
+            out.at[y, 1 - x, o, pl.ds(0, 2)],
+            out.at[1 - y, x, o, pl.ds(2, 2)],
+            out.at[y, 1 - x, o, pl.ds(2, 2)],
+            out.at[1 - y, x, o, pl.ds(0, 2)],
+            out.at[1 - y, 1 - x, o, pl.ds(2, 2)],
+            out.at[1 - y, 1 - x, o, pl.ds(0, 2)],
+        ]
+        for k, ref in enumerate(arrivals):
+            self.arrived(ref, self.cs.at[i, k], self.cr.at[i, k])
+
+
+def gather_kernel(count, *refs):
+    here = place()
+    sender = Sender()
+    rest = refs[2 * count :]
+    gather = Gather(here, sender, refs[:count], refs[count : 2 * count], rest[:8], rest[8])
+    greet(here)
+    gather.start()
+    for t in range(count + 2):
+        if t < count:
+            gather.stage1(t)
+        if 0 <= t - 1 < count:
+            gather.stage2(t - 1)
+        if 0 <= t - 2 < count:
+            gather.stage3(t - 2)
+    for i in range(count):
+        gather.finish(i)
+    sender.drain()
+
+
+def gather_all(shards):
+    count = len(shards)
+    return pl.pallas_call(
+        lambda *refs: gather_kernel(count, *refs),
+        out_shape=tuple(jax.ShapeDtypeStruct((2, 2, 2, 4) + s.shape, s.dtype) for s in shards),
+        in_specs=[pl.BlockSpec(memory_space=pltpu.VMEM)] * count,
+        out_specs=tuple([pl.BlockSpec(memory_space=pl.ANY)] * count),
+        scratch_shapes=Gather.scratch(count),
+        compiler_params=pltpu.CompilerParams(collective_id=1, has_side_effects=True),
+        name="gather_weights",
+    )(*shards)
+
+
+class Scatter:
+    SEMAPHORES = ((), (), (), (2,), (2,), (2,), (2,), (3,), (3,))
+    LEADING = ((2, 2, 4), (2, 2, 4), (2, 2), (2, 2), (2,), (2,), (3,))
+
+    def __init__(self, here, sender, part, out, buffers, semaphores):
+        self.here, self.sender, self.part, self.out = here, sender, part, out
+        n = len(part)
+        self.acc, self.r0, self.r1a, self.r1b, self.r2a, self.r2b, self.r3 = (
+            buffers[k * n : (k + 1) * n] for k in range(7)
+        )
+        self.local, self.cs, self.cr, self.s1, self.v1, self.s2, self.v2, self.s3, self.v3 = semaphores
+        y, x, c, z = here
+        self.sib = device_at(y, x, 1 - c, z)
+        self.xn = device_at(y, 1 - x, c, z)
+        self.yn = device_at(1 - y, x, c, z)
+
+    @staticmethod
+    def scratch(blocks):
+        n = len(blocks)
+        kinds = [pltpu.VMEM(lead + b, BF16) for lead in Scatter.LEADING for b in blocks]
+        return kinds + [pltpu.SemaphoreType.DMA((n,) + k) for k in Scatter.SEMAPHORES]
+
+    def load(self, i):
+        c = self.here[2]
+        return pltpu.make_async_copy(self.part[i].at[:, :, c], self.acc[i], self.local.at[i])
+
+    def hop(self, i, stage, k):
+        y, x, c, z = self.here
+        acc = self.acc[i]
+        if stage == 0:
+            return (self.part[i].at[:, :, 1 - c], self.r0[i], self.cs.at[i], self.cr.at[i], self.sib)
+        if stage == 1:
+            if k == 0:
+                return (acc.at[1 - y, :, pl.ds(0, 2)], self.r1a[i], self.s1.at[i, 0], self.v1.at[i, 0], self.yn)
+            return (acc.at[:, 1 - x, pl.ds(2, 2)], self.r1b[i], self.s1.at[i, 1], self.v1.at[i, 1], self.xn)
+        if stage == 2:
+            if k == 0:
+                return (acc.at[y, 1 - x, pl.ds(0, 2)], self.r2a[i], self.s2.at[i, 0], self.v2.at[i, 0], self.xn)
+            return (acc.at[1 - y, x, pl.ds(2, 2)], self.r2b[i], self.s2.at[i, 1], self.v2.at[i, 1], self.yn)
+        there = (z + k + 1) % 4
+        return (acc.at[y, x, there], self.r3[i].at[k], self.s3.at[i, k], self.v3.at[i, k], device_at(y, x, c, there))
+
+    def send(self, i, stage, k):
+        self.sender.go(*self.hop(i, stage, k))
+
+    def wait(self, i, stage, k):
+        remote(*self.hop(i, stage, k)).wait_recv()
+
+    def start(self):
+        for i in range(len(self.part)):
+            self.send(i, 0, 0)
+
+    def stage1(self, i):
+        acc, r0 = self.acc[i], self.r0[i]
+        self.load(i).wait()
+        self.wait(i, 0, 0)
+
+        def add(k, _):
+            a, b, q = k // 8, (k // 4) % 2, k % 4
+            acc[a, b, q] = acc[a, b, q] + r0[a, b, q]
+            return 0
+
+        lax.fori_loop(0, 16, add, 0)
+        self.send(i, 1, 0)
+        self.send(i, 1, 1)
+
+    def stage2(self, i):
+        y, x, c, z = self.here
+        acc, r1a, r1b = self.acc[i], self.r1a[i], self.r1b[i]
+        self.wait(i, 1, 0)
+        self.wait(i, 1, 1)
+
+        def add(k, _):
+            a, q = k // 2, k % 2
+            acc[y, a, q] = acc[y, a, q] + r1a[a, q]
+            acc[a, x, q + 2] = acc[a, x, q + 2] + r1b[a, q]
+            return 0
+
+        lax.fori_loop(0, 4, add, 0)
+        self.send(i, 2, 0)
+        self.send(i, 2, 1)
+
+    def stage3(self, i):
+        y, x, c, z = self.here
+        acc = self.acc[i]
+        self.wait(i, 2, 0)
+        self.wait(i, 2, 1)
+        for q in range(2):
+            acc[y, x, q] = acc[y, x, q] + self.r2a[i][q]
+            acc[y, x, q + 2] = acc[y, x, q + 2] + self.r2b[i][q]
+        for k in (1, 0, 2):
+            self.send(i, 3, k)
+
+    def stage4(self, i):
+        y, x, c, z = self.here
+        for k in range(3):
+            self.wait(i, 3, k)
+        acc, r3 = self.acc[i], self.r3[i]
+        self.out[i][...] = (acc[y, x, z].astype(F32) + r3[0].astype(F32)) + (
+            r3[1].astype(F32) + r3[2].astype(F32)
+        )
+
+
+def scatter_kernel(n, *refs):
+    here = place()
+    sender = Sender()
+    part, small = refs[:n], refs[n]
+    out, small_out = refs[n + 1 : 2 * n + 1], refs[2 * n + 1]
+    rest = refs[2 * n + 2 :]
+    scatter = Scatter(here, sender, part, out, rest[: 7 * n], rest[7 * n : 7 * n + 9])
+    gather = Gather(here, sender, [small], [small_out], rest[7 * n + 9 : -1], rest[-1])
+    for i in range(n):
+        scatter.load(i).start()
+    greet(here)
+    gather.start()
+    scatter.start()
+    for t in range(n + 3):
+        if t < n:
+            scatter.stage1(t)
+        if 0 <= t - 1 < n:
+            scatter.stage2(t - 1)
+        if 0 <= t - 2 < n:
+            scatter.stage3(t - 2)
+        if 0 <= t - 3 < n:
+            scatter.stage4(t - 3)
+        if t < 4:
+            (gather.stage1, gather.stage2, gather.stage3, gather.finish)[t](0)
+    sender.drain()
+
+
+def scatter_all(parts, small):
+    n = len(parts)
+    blocks = [p.shape[4:] for p in parts]
+    any_space = pl.BlockSpec(memory_space=pl.ANY)
+    vmem = pl.BlockSpec(memory_space=pltpu.VMEM)
+    return pl.pallas_call(
+        lambda *refs: scatter_kernel(n, *refs),
+        out_shape=tuple(jax.ShapeDtypeStruct(b, F32) for b in blocks)
+        + (jax.ShapeDtypeStruct((2, 2, 2, 4) + small.shape, small.dtype),),
+        in_specs=[any_space] * n + [vmem],
+        out_specs=tuple([vmem] * n + [any_space]),
+        scratch_shapes=Scatter.scratch(blocks) + Gather.scratch(1),
+        compiler_params=pltpu.CompilerParams(
+            collective_id=2, has_side_effects=True, vmem_limit_bytes=60 << 20
+        ),
+        name="scatter_gradients",
+    )(*parts, small)
+
+
+def gather_plain(shards):
+    return tuple(lax.all_gather(s, AXES, axis=0) for s in shards)
+
+
+def scatter_plain(parts, small):
+    devices = lax.axis_size(AXES)
+    sums = tuple(
+        lax.psum_scatter(p.reshape((devices,) + p.shape[-2:]), AXES, scatter_dimension=0, tiled=True)[
+            0
+        ].astype(F32)
+        for p in parts
+    )
+    return sums + (lax.all_gather(small, AXES, axis=0),)
+
 
 def per_device(latents, buckets, step_ids, qs, ps, qt, pt, up, down, ada, biases, cotangent):
     devices = lax.axis_size(AXES)
@@ -85,23 +419,26 @@
     tokens = frames * spatial
     rows = D // devices
 
-    steps = lax.all_gather(step_ids[:, 0], AXES, axis=0, tiled=True)
-    condition = timestep_condition(steps)
+    known = lax.axis_size("wide") == 8 and lax.axis_size("narrow") == 4
+    gather, scatter = (gather_all, scatter_all) if known else (gather_plain, scatter_plain)
+
     ada_columns = lax.all_to_all(
         ada.reshape(rows, 9 * D), AXES, split_axis=1, concat_axis=0, tiled=True
     )
+    own_bias = jnp.pad(biases, (0, D - biases.shape[0]))[None]
+    small = jnp.concatenate([timestep_condition(step_ids[:, 0]), own_bias], axis=0)
+    shards = [small] + [w.reshape(rows, -1) for w in (qs, ps, qt, pt, up)] + [down.reshape(-1, D)]
+    small, *gathered = gather(shards)
+    w_qs, w_ps, w_qt, w_pt, w_up = (w.reshape(D, -1) for w in gathered[:5])
+    w_down = gathered[5].reshape(-1, D)
+    small = small.reshape(devices, micro + 1, D)
+    condition = small[:, :micro].reshape(devices * micro, D)
+    bias = small[:, micro, : biases.shape[0]].reshape(-1).astype(F32)
     modulation = lax.all_to_all(
         dot(condition, ada_columns), AXES, split_axis=0, concat_axis=1, tiled=True
     )
-    bias = lax.all_gather(biases, AXES, axis=0, tiled=True).astype(F32)
     modulation = (modulation + bias[: 9 * D]).reshape(micro, 9, 1, D)
     b_up, b_down = bias[9 * D : 9 * D + FF], bias[9 * D + FF :]
-
-    wide_shard = jnp.concatenate([w.reshape(rows, -1) for w in (qs, ps, qt, pt, up)], axis=1)
-    wide = lax.all_gather(wide_shard, AXES, axis=0, tiled=True)
-    w_down = lax.all_gather(down.reshape(-1, D), AXES, axis=0, tiled=True)
-    cuts = [3 * D, 4 * D, 7 * D, 8 * D]
-    w_qs, w_ps, w_qt, w_pt, w_up = jnp.split(wide, cuts, axis=1)
 
     positions = jnp.arange(tokens)
     frame, place = positions // spatial, positions % spatial
@@ -154,10 +491,18 @@
     dv, dsh1, dsc1 = norm_back(dh1, n1, r1, sc1)
     latents_grad = d1 + dv
 
-    dmod = jnp.concatenate([dsh1, dsc1, dga1, dsh2, dsc2, dga2, dsh3, dsc3, dga3], axis=-1)
-    small = jnp.concatenate([dmod.reshape(1, -1), db_up[None], db_down[None]], axis=-1)
-    small = lax.all_gather(small.astype(BF16), AXES, axis=0, tiled=True)
-    dmod_all = small[:, : micro * 9 * D].reshape(devices * micro, 9 * D)
+    dmod = jnp.stack([dsh1, dsc1, dga1, dsh2, dsc2, dga2, dsh3, dsc3, dga3], axis=1)
+    small = jnp.concatenate(
+        [dmod.reshape(micro * 9, D), db_up.reshape(-1, D), db_down.reshape(-1, D)], axis=0
+    ).astype(BF16)
+    parts = [
+        part.astype(BF16).reshape(tuple(gathered[i].shape))
+        for i, part in ((5, dw_down), (4, dw_up), (3, dw_pt), (2, dw_qt), (1, dw_ps), (0, dw_qs))
+    ]
+    ddown, dup, dpt, dqt, dps, dqs, small = scatter(parts, small)
+    flat = tuple(part.reshape(-1) for part in (dqs, dps, dqt, dpt, dup))
+    small = small.reshape(devices, -1, D)
+    dmod_all = small[:, : micro * 9].reshape(devices * micro, 9 * D)
     me = lax.axis_index(AXES)
     my_condition = lax.dynamic_slice_in_dim(condition, me * rows, rows, axis=1)
     dw_ada = lax.dot_general(
@@ -166,15 +511,11 @@
     db = jnp.concatenate(
         [
             jnp.sum(dmod_all.astype(F32), axis=0),
-            jnp.sum(small[:, micro * 9 * D :].astype(F32), axis=0),
+            jnp.sum(small[:, micro * 9 :].astype(F32), axis=0).reshape(-1),
         ]
     )
     db = lax.dynamic_slice_in_dim(db, me * biases.shape[0], biases.shape[0])
 
-    dwide = jnp.concatenate([w.astype(BF16) for w in (dw_qs, dw_ps, dw_qt, dw_pt, dw_up)], axis=1)
-    dwide = lax.psum_scatter(dwide, AXES, scatter_dimension=0, tiled=True).astype(F32)
-    ddown = lax.psum_scatter(dw_down.astype(BF16), AXES, scatter_dimension=0, tiled=True).astype(F32)
-    flat = tuple(part.reshape(-1) for part in jnp.split(dwide, cuts, axis=1))
     shape = latents.shape
     return (
         output.reshape(shape),

time: 645 us -> 418 us (0.65)
  waiting for transfers between devices: 302 us -> 6.27 us
  Pallas kernels: 0 us -> 201 us
  blocking collectives: 86.5 us -> 0 us
  matrix products: 141 us -> 116 us
  between operations: 15.5 us -> 1.77 us
  local copies, waits for them, and re-layouts: 62.7 us -> 51.7 us
  starting transfers between devices: 11.9 us -> 19 us
    reduce_scatter x2 -> x0, waiting for transfers between devices: 273 us -> none  [the longest x1 166 us: per_device(): lax.psum_scatter(dwide, AXES, scatter_dimension=0, tiled=True).astype(F32)]
    pallas_call x0 -> x2, Pallas kernels: none -> 201 us  [the longest x1 102 us: scatter_all(): pl.pallas_call(lambda *refs: scatter_kernel(n, *refs), out_shape=tuple((j...]
    unnamed x2 -> x0, blocking collectives: 86.5 us -> none
    all_gather x3 -> x0, waiting for transfers between devices: 29.1 us -> none  [the longest x1 12.8 us: per_device(): small = lax.all_gather(small.astype(BF16), AXES, axis=0, tiled=True)]
    unnamed x171 -> x105, local copies, waits for them, and re-layouts: 12.2 us -> 3.5 us
    dot_general x7, matrix products: 28 us -> 20.2 us  [dot(): return jnp.dot(a, b, preferred_element_type=F32)]
    all_to_all x1, starting transfers between devices: 4.37 us -> 11.7 us  [per_device(): lax.all_to_all(dot(condition, ada_columns), AXES, split_axis=0, concat_ax...]
  transfers between devices with their start and end apart: 7 -> 2, of which waited for: 5 -> 1; matrix products, arithmetic and copies ran while one was open for 17% -> 3% of each run, Pallas kernels for 0% -> 24%
where the time goes in v2:
time: 418 us; the launch traced here: 412 us
  Pallas kernels  201 us (48%)
  matrix products  116 us (28%)
  local copies, waits for them, and re-layouts  51.7 us (12%)
  starting transfers between devices  19 us (5%)
  other arithmetic  16.1 us (4%)
  waiting for transfers between devices  6.27 us (2%)
    pallas_call x1, Pallas kernels, scatter_all(): pl.pallas_call(lambda *refs: scatter_kernel(n, *refs), out_shape=tuple((j...  102 us
    pallas_call x1, Pallas kernels, gather_all(): pl.pallas_call(lambda *refs: gather_kernel(count, *refs), out_shape=tuple...  99 us
    dot_general x7, matrix products, dot(): return jnp.dot(a, b, preferred_element_type=F32)  20.2 us
    all_to_all x1, starting transfers between devices, per_device(): lax.all_to_all(dot(condition, ada_columns), AXES, split_axis=0, concat_ax...  11.7 us
    split x8, local copies, waits for them, and re-layouts, attention(): q, k, v = (heads(part) for part in jnp.split(packed, 3, axis=-1))  11.6 us
    dot_general x2, matrix products, attention_back(): jnp.einsum('ble,de->bld', packed, qkv_w, preferred_element_type=F32)  11.4 us
    sub x2, matrix products, attention(): soft = jax.nn.softmax(scores, axis=-1)  10.7 us
    dot_general x2, matrix products, attention_back(): jnp.einsum('bhqk,bqhd->bkhd', soft.astype(BF16), ctx, preferred_element_t...  10.3 us
  transfers between devices with their start and end apart: 2, of which 1 were waited for; matrix products, arithmetic and copies ran while one was open for 3% of the time, Pallas kernels for 24%

profile of v2, /device:TPU:0, one launch (start us, length us, event | category | flops | bytes accessed | tf_op | source)
XLA Modules:
  0.0 411.7 jit_solution(10034871578208646587)
XLA Ops:
  4.0 7.3 %all-to-all-start = ((bf16[24,32,216]{2,0,1:T(8,128)(2,1)}), bf16[24,32,216]{2,0,1:T(8,128)(2,1)S(1)}, u32[]{:S(2)}, u32[]{:S(2)}) async-start(bf16[24,32,216]{2,0,1:T(8,128)(2,1)} %copy.98), calls=%async_computation | async-start | bytes 786432 | tf_op jit(solution)/shard_map/all_to_all | solution.py:425
  18.7 99.0 %gather_weights.1 = (bf16[2,2,2,4,3,768]{5,4,3,2,1,0:T(4,128)(2,1)}, bf16[2,2,2,4,24,2304]{5,4,3,2,1,0:T(8,128)(2,1)}, bf16[2,2,2,4,24,768]{5,4,3,2,1,0:T(8,128)...) custom-call(bf16[3,768]{1,0:T(4,128)(2,1)} %pad_maximum_fusion.8.ref, ...), custom_call_target="tpu_custom_call" | custom-call | tf_op jit(solution)/shard_map/gather_weights/pallas_call | solution.py:240
  121.7 11.7 %all-to-all-start.1 = ((f32[32,2,216]{2,1,0:T(2,128)}), f32[32,2,216]{2,1,0:T(2,128)S(1)}, u32[]{:S(2)}, u32[]{:S(2)}) async-start(f32[32,2,216]{2,1,0:T(2,128)} %copy.100), calls=%async_computation.1 | async-start | bytes 131072 | tf_op jit(solution)/shard_map/all_to_all | solution.py:437
  134.5 6.3 %all-to-all-done.1 = f32[32,2,216]{2,1,0:T(2,128)S(1)} async-done(((f32[32,2,216]{2,1,0:T(2,128)}), f32[32,2,216]{2,1,0:T(2,128)S(1)}, u32[]{:S(2)}, u32[]{:S(2)}) %all-to-all-start.1) | async-done | bytes 55328 | tf_op jit(solution)/shard_map/all_to_all | solution.py:437
  141.3 4.0 convolution_convert_fusion.1
  149.5 4.8 %fusion.91 = (f32[2,12,256]{2,1,0:T(8,128)S(1)}, f32[2,12,256,256]{2,3,1,0:T(8,128)}) fusion(pred[2,256,256]{1,2,0:T(8,128)(4,1)S(1)} %broadcast_and_fusion, bf16[2,256,12,64]{1,3,2,0:T(8,128)(2,1)S(1)} %bitcast.229, bf16[2,256,12,64]{1,3,2,0:T(8,128)(2,1)S(1)} %bitcast.227), kind=kOutput, calls=%fused_computation.200 | convolution fusion | flops 207618304 | bytes 8019968 | tf_op jit(solution)/shard_map/sub | solution.py:59
  154.4 3.5 fusion.43
  165.8 2.3 copy.109
  168.1 2.3 copy.108
  170.3 5.9 %fusion.92 = (f32[2,12,256]{2,1,0:T(8,128)S(1)}, f32[2,12,256,256]{2,3,1,0:T(8,128)}) fusion(pred[256,256]{0,1:T(8,128)(4,1)S(1)} %broadcast_compare_fusion, bf16[2,256,12,64]{1,3,2,0:T(8,128)(2,1)} %bitcast.233, bf16[2,256,12,64]{1,3,2,0:T(8,128)(2,1)S(1)} %bitcast.231), kind=kOutput, calls=%fused_computation.201 | convolution fusion | flops 207618304 | bytes 7954432 | tf_op jit(solution)/shard_map/sub | solution.py:59
  176.2 4.0 fusion.49
  181.9 4.9 %fusion.65 = f32[2,256,3072]{2,1,0:T(8,128)S(1)} fusion(bf16[768,3072,1]{1,0,2:T(8,128)(2,1)} %bitcast.275, f32[2,256,768]{2,1,0:T(8,128)S(1)} %get-tuple-element.89, f32[2,768]{1,0:T(2,128)S(1)} %get-tuple-element.130, f32[2,768]{1,0:T(2,128)S(1)} %get-tuple-element.131, f32[2,256]{1,0:T(2,128)S(1)} %add_rsqrt_fusion.1, ...), kind=kOutput, calls=%fused_computation.134 | convolution fusion | flops 2417885184 | bytes 12599296 | tf_op jit(solution)/shard_map/dot_general | solution.py:47
  186.8 6.6 %fusion.93 = (bf16[3072]{0:T(1024)(128)(2,1)S(1)}, bf16[2,256,3072]{2,1,0:T(8,128)(2,1)S(1)}) fusion(f32[2,256,3072]{2,1,0:T(8,128)S(1)} %fusion.65, f32[3072]{0:T(1024)S(1)} %slice.81, bf16[2,256,768]{2,1,0:T(8,128)(2,1)S(1)} %bitcast.257, bf16[3072,768,1]{1,0,2:T(8,128)(2,1)S(1)} %bitcast.273), kind=kOutput, calls=%fused_computation.202 | convolution fusion | flops 2450519040 | bytes 14960640 | tf_op jit(solution)/shard_map/bsd,kd->bsk/dot_general | solution.py:476
  193.5 3.1 multiply_reduce_fusion.3
  196.6 4.8 %bitcast_convert_fusion = bf16[768,3072]{1,0:T(8,128)(2,1)} fusion(bf16[2,256,3072]{2,1,0:T(8,128)(2,1)S(1)} %get-tuple-element.129, f32[2,256,768]{2,1,0:T(8,128)S(1)} %get-tuple-element.89, f32[2,768]{1,0:T(2,128)S(1)} %get-tuple-element.130, f32[2,768]{1,0:T(2,128)S(1)} %get-tuple-element.131, f32[2,256]{1,0:T(2,128)S(1)} %add_rsqrt_fusion.1, ...), kind=kOutput, calls=%fused_computation.2 | convolution fusion | flops 2420244480 | bytes 9453568 | tf_op jit(solution)/shard_map/bsd,bsk->dk/dot_general | solution.py:479
  201.4 6.0 %multiply_reduce_fusion.2 = (bf16[2,768]{1,0:T(2,128)(2,1)S(1)}, bf16[2,256,768]{2,1,0:T(8,128)(2,1)}, bf16[2,768]{1,0:T(2,128)(2,1)S(1)}, f32[2,256,768]{2,1,0:T(8,128)S(1)}, bf16[2,256,768]{2,1,0:T(8,128)(2,1)}) fusion(bf16[2,1,16,16,768]{4,3,2,1,0:T(8,128)(2,1)S(1)} %copy-done.17, f32[2,256]{1,0:T(2,128)S(1)} %get-tuple-element.86, f32[768]{0:T(1024)S(1)} %slice.82, ...), kind=kOutput, calls=%fused_computation.64 | convolution fusion | flops 2439902208 | bytes 19704832 | tf_op jit(solution)/shard_map/dot_general | solution.py:47
  210.9 2.3 copy.113
  213.2 5.2 %fusion.52 = bf16[2,12,64,256]{3,2,1,0:T(8,128)(2,1)} fusion(bf16[2,256,12,64]{1,3,2,0:T(8,128)(2,1)} %bitcast.258, f32[2,12,256,256]{2,3,1,0:T(8,128)} %get-tuple-element.119, f32[2,12,256]{2,1,0:T(8,128)S(1)} %get-tuple-element.118), kind=kOutput, calls=%fused_computation.102 | convolution fusion | flops 204865536 | bytes 7888896 | tf_op jit(solution)/shard_map/bhqk,bqhd->bkhd/dot_general | solution.py:69
  218.4 6.7 %multiply_reduce_fusion.1 = (f32[2,12,256]{2,1,0:T(8,128)S(1)}, f32[2,12,256,256]{2,3,1,0:T(8,128)}) fusion(f32[2,12,256,256]{2,3,1,0:T(8,128)} %get-tuple-element.119, f32[2,12,256]{2,1,0:T(8,128)S(1)} %get-tuple-element.118, bf16[2,256,12,64]{1,3,2,0:T(8,128)(2,1)S(1)} %bitcast.259, bf16[2,256,12,64]{1,3,2,0:T(8,128)(2,1)S(1)} %bitcast.254), kind=kOutput, calls=%fused_computation.18 | convolution fusion | flops 206039040 | bytes 14204928 | tf_op jit(solution)/shard_map/bqhd,bkhd->bhqk/dot_general | solution.py:70
  225.1 4.4 %multiply_convert_fusion.1 = bf16[2,12,256,256]{2,3,1,0:T(8,128)(2,1)S(1)} fusion(f32[2,12,256,256]{2,3,1,0:T(8,128)} %get-tuple-element.123, f32[2,12,256]{2,1,0:T(8,128)S(1)} %get-tuple-element.122, f32[2,12,256,256]{2,3,1,0:T(8,128)S(1)} %bitcast.220, f32[2,12,256]{2,1,0:T(8,128)S(1)} %get-tuple-element.118), kind=kLoop, calls=%fused_computation.17 | loop fusion | flops 6291456 | bytes 15777792 | tf_op jit(solution)/shard_map/convert_element_type | solution.py:72
  233.0 2.4 copy.119
  235.3 2.3 copy.117
  238.8 5.3 %multiply_reduce_fusion.5 = (bf16[2,768]{1,0:T(2,128)(2,1)S(1)}, f32[2,256]{1,0:T(2,128)S(1)}, f32[2,256]{1,0:T(2,128)S(1)}, bf16[2,768]{1,0:T(2,128)(2,1)S(1)}, f32[2,256,768]{2,1,0:T(8,128)S(1)}) fusion(f32[2,256,768]{2,1,0:T(8,128)S(1)} %get-tuple-element.91, f32[2,256]{1,0:T(2,128)S(1)} %add_rsqrt_fusion.2, f32[2,256]{1,0:T(2,128)S(1)} %broadcast_multiply_fusion.8, ...), kind=kOutput, calls=%fused_computation.67 | convolution fusion | flops 1822552064 | bytes 9064448 | tf_op jit(solution)/shard_map/ble,de->bld/dot_general | solution.py:79
  244.2 4.1 bitcast_convert_fusion.3
  253.1 2.3 copy.120
  255.4 5.2 %fusion.46 = bf16[2,12,64,256]{3,2,1,0:T(8,128)(2,1)} fusion(bf16[2,256,12,64]{1,3,2,0:T(8,128)(2,1)} %bitcast.260, f32[2,12,256,256]{2,3,1,0:T(8,128)} %get-tuple-element.116, f32[2,12,256]{2,1,0:T(8,128)S(1)} %get-tuple-element.115), kind=kOutput, calls=%fused_computation.100 | convolution fusion | flops 204865536 | bytes 7888896 | tf_op jit(solution)/shard_map/bhqk,bqhd->bkhd/dot_general | solution.py:69
  263.3 2.3 multiply_convert_fusion.4
  266.7 8.8 %bitcast_convert_fusion.1 = bf16[3072,768]{1,0:T(8,128)(2,1)} fusion(bf16[2,256,768]{2,1,0:T(8,128)(2,1)S(1)} %copy-done.36, f32[2,256,3072]{2,1,0:T(8,128)} %copy-done.35, f32[3072]{0:T(1024)S(1)} %slice.81), kind=kOutput, calls=%fused_computation.3 | convolution fusion | flops 2434007040 | bytes 11808768 | tf_op jit(solution)/shard_map/bsk,bsd->kd/dot_general | solution.py:475
  278.4 6.1 %fusion.34 = (bf16[2,768]{1,0:T(2,128)(2,1)S(1)}, f32[2,256]{1,0:T(2,128)S(1)}, f32[2,256]{1,0:T(2,128)S(1)}, bf16[2,768]{1,0:T(2,128)(2,1)S(1)}, bf16[2,256,768]{2,1,0:T(8,128)(2,1)}, /*index=5*/f32[2,256,768]{2,1,0:T(8,128)}) fusion(bf16[2,1,16,16,768]{4,3,2,1,0:T(8,128)(2,1)S(1)} %copy-done, f32[2,256]{1,0:T(2,128)S(1)} %div.92, ...), kind=kOutput, calls=%fused_computation.63 | convolution fusion | flops 1824124928 | bytes 9070592 | tf_op jit(solution)/shard_map/ble,de->bld/dot_general | solution.py:79
  284.6 4.9 %bitcast_convert_fusion.2 = bf16[768,2304]{1,0:T(8,128)(2,1)} fusion(bf16[2,256,768]{2,1,0:T(8,128)(2,1)} %get-tuple-element.102, bf16[2,256,768]{2,1,0:T(8,128)(2,1)S(1)} %copy.126, bf16[2,256,768]{2,1,0:T(8,128)(2,1)S(1)} %copy.125, bf16[2,256,768]{2,1,0:T(8,128)(2,1)S(1)} %copy-done.21), kind=kOutput, calls=%fused_computation.6 | convolution fusion | flops 1820786688 | bytes 6684672 | tf_op jit(solution)/shard_map/bld,ble->de/dot_general | solution.py:78
  290.2 102.1 %scatter_gradients.1 = (f32[96,768]{1,0:T(8,128)}, f32[24,3072]{1,0:T(8,128)}, f32[24,768]{1,0:T(8,128)}, f32[24,2304]{1,0:T(8,128)}, f32[24,768]{1,0:T(8,128)},...) custom-call(bf16[2,2,2,4,96,768]{5,4,3,2,1,0:T(8,128)(2,1)} %bitcast.222, ...), custom_call_target="tpu_custom_call" | custom-call | tf_op jit(solution)/shard_map/scatter_gradients/pallas_call | solution.py:386
  407.7 3.1 fusion.31
  (209 shorter events, 66.1 us)
Async XLA Ops:
  0.6 13.5 %copy-start.32 = (bf16[18432]{0:T(1024)(128)(2,1)S(1)}, bf16[18432]{0:T(1024)(128)(2,1)}, u32[]{:S(2)}) copy-start(bf16[18432]{0:T(1024)(128)(2,1)} %param.18) | copy-start | bytes 110596
  0.7 14.1 %copy-start.30 = (bf16[55296]{0:T(1024)(128)(2,1)S(1)}, bf16[55296]{0:T(1024)(128)(2,1)}, u32[]{:S(2)}) copy-start(bf16[55296]{0:T(1024)(128)(2,1)} %param.15) | copy-start | bytes 331780
  0.7 14.9 %copy-start.31 = (bf16[55296]{0:T(1024)(128)(2,1)S(1)}, bf16[55296]{0:T(1024)(128)(2,1)}, u32[]{:S(2)}) copy-start(bf16[55296]{0:T(1024)(128)(2,1)} %param.17) | copy-start | bytes 331780
  0.7 15.7 %copy-start.28 = (bf16[73728]{0:T(1024)(128)(2,1)S(1)}, bf16[73728]{0:T(1024)(128)(2,1)}, u32[]{:S(2)}) copy-start(bf16[73728]{0:T(1024)(128)(2,1)} %param.19) | copy-start | bytes 442372
  0.7 16.4 %copy-start.29 = (bf16[73728]{0:T(1024)(128)(2,1)S(1)}, bf16[73728]{0:T(1024)(128)(2,1)}, u32[]{:S(2)}) copy-start(bf16[73728]{0:T(1024)(128)(2,1)} %param.20) | copy-start | bytes 442372
  0.7 119.0 %copy-start.34 = (s32[2,1]{0,1:T(1,128)S(1)}, s32[2,1]{0,1:T(1,128)}, u32[]{:S(2)}) copy-start(s32[2,1]{0,1:T(1,128)} %param.13) | copy-start | bytes 28
  0.7 119.0 %copy-start = (bf16[2,1,16,16,768]{4,3,2,1,0:T(8,128)(2,1)S(1)}, bf16[2,1,16,16,768]{4,3,2,1,0:T(8,128)(2,1)}, u32[]{:S(2)}) copy-start(bf16[2,1,16,16,768]{4,3,2,1,0:T(8,128)(2,1)} %param.12) | copy-start | bytes 2359300
  4.0 116.9 %all-to-all-start = ((bf16[24,32,216]{2,0,1:T(8,128)(2,1)}), bf16[24,32,216]{2,0,1:T(8,128)(2,1)S(1)}, u32[]{:S(2)}, u32[]{:S(2)}) async-start(bf16[24,32,216]{2,0,1:T(8,128)(2,1)} %copy.98), calls=%async_computation | async-start | bytes 786432 | tf_op jit(solution)/shard_map/all_to_all | solution.py:425
  121.7 19.0 %all-to-all-start.1 = ((f32[32,2,216]{2,1,0:T(2,128)}), f32[32,2,216]{2,1,0:T(2,128)S(1)}, u32[]{:S(2)}, u32[]{:S(2)}) async-start(f32[32,2,216]{2,1,0:T(2,128)} %copy.100), calls=%async_computation.1 | async-start | bytes 131072 | tf_op jit(solution)/shard_map/all_to_all | solution.py:437
  146.6 7.7 %copy-start.6 = (bf16[2,256,768]{1,2,0:T(8,128)(2,1)}, bf16[2,256,768]{1,2,0:T(8,128)(2,1)S(1)}, u32[]{:S(2)}) copy-start(bf16[2,256,768]{1,2,0:T(8,128)(2,1)S(1)} %copy.105) | copy-start | bytes 2359300
  148.4 6.0 %copy-start.8 = (bf16[2,256,768]{1,2,0:T(8,128)(2,1)}, bf16[2,256,768]{1,2,0:T(8,128)(2,1)S(1)}, u32[]{:S(2)}) copy-start(bf16[2,256,768]{1,2,0:T(8,128)(2,1)S(1)} %copy.104) | copy-start | bytes 2359300
  149.5 4.8 %copy-start.18 = (bf16[2,256,768]{1,2,0:T(8,128)(2,1)S(1)}, bf16[2,256,768]{1,2,0:T(8,128)(2,1)}, u32[]{:S(2)}) copy-start(bf16[2,256,768]{1,2,0:T(8,128)(2,1)} %copy.103) | copy-start | bytes 2359300
  181.6 5.3 %slice-start.4 = ((s8[4718592]{0:T(1024)(128)(4,1)}), s8[4194304]{0:T(1024)(128)(4,1)S(1)}, s32[]{:S(2)}) async-start(s8[4718592]{0:T(1024)(128)(4,1)} %bitcast.271), calls=%async_computation.6 | async-start | bytes 8388608
  181.9 4.9 %slice-start.5 = ((s8[4718592]{0:T(1024)(128)(4,1)}), s8[524288]{0:T(1024)(128)(4,1)S(1)}, s32[]{:S(2)}) async-start(s8[4718592]{0:T(1024)(128)(4,1)} %bitcast.271), calls=%async_computation.7 | async-start | bytes 1048576
  181.9 11.6 %slice-start.6 = ((s8[4718592]{0:T(1024)(128)(4,1)}), s8[4194304]{0:T(1024)(128)(4,1)S(1)}, s32[]{:S(2)}) async-start(s8[4718592]{0:T(1024)(128)(4,1)} %bitcast.276), calls=%async_computation.8 | async-start | bytes 8388608
  186.8 14.6 %copy-start.35 = (f32[2,256,3072]{2,1,0:T(8,128)}, f32[2,256,3072]{2,1,0:T(8,128)S(1)}, u32[]{:S(2)}) copy-start(f32[2,256,3072]{2,1,0:T(8,128)S(1)} %fusion.65) | copy-start | bytes 18874372
  186.8 6.6 %slice-start.7 = ((s8[4718592]{0:T(1024)(128)(4,1)}), s8[524288]{0:T(1024)(128)(4,1)S(1)}, s32[]{:S(2)}) async-start(s8[4718592]{0:T(1024)(128)(4,1)} %bitcast.276), calls=%async_computation.9 | async-start | bytes 1048576
  213.2 5.2 %copy-start.20 = (bf16[2,256,768]{1,2,0:T(8,128)(2,1)S(1)}, bf16[2,256,768]{1,2,0:T(8,128)(2,1)}, u32[]{:S(2)}) copy-start(bf16[2,256,768]{1,2,0:T(8,128)(2,1)} %copy.108) | copy-start | bytes 2359300
  213.2 5.2 %copy-start.25 = (bf16[2,256,768]{1,2,0:T(8,128)(2,1)S(1)}, bf16[2,256,768]{1,2,0:T(8,128)(2,1)}, u32[]{:S(2)}) copy-start(bf16[2,256,768]{1,2,0:T(8,128)(2,1)} %copy.113) | copy-start | bytes 2359300
  213.2 11.8 %slice-start.2 = ((s8[6291456]{0:T(1024)(128)(4,1)}), s8[4194304]{0:T(1024)(128)(4,1)S(1)}, s32[]{:S(2)}) async-start(s8[6291456]{0:T(1024)(128)(4,1)} %bitcast.219), calls=%async_computation.4 | async-start | bytes 8388608
  218.4 6.7 %slice-start.3 = ((s8[6291456]{0:T(1024)(128)(4,1)}), s8[2097152]{0:T(1024)(128)(4,1)S(1)}, s32[]{:S(2)}) async-start(s8[6291456]{0:T(1024)(128)(4,1)} %bitcast.219), calls=%async_computation.5 | async-start | bytes 4194304
  233.0 4.7 %copy-start.10 = (bf16[2,12,64,256]{3,2,1,0:T(8,128)(2,1)S(1)}, bf16[2,12,64,256]{3,2,1,0:T(8,128)(2,1)}, u32[]{:S(2)}) copy-start(bf16[2,12,64,256]{3,2,1,0:T(8,128)(2,1)} %multiply_convert_fusion.7) | copy-start | bytes 2359300
  238.8 5.4 %copy-start.22 = (bf16[2,256,768]{2,1,0:T(8,128)(2,1)S(1)}, bf16[2,256,768]{2,1,0:T(8,128)(2,1)}, u32[]{:S(2)}) copy-start(bf16[2,256,768]{2,1,0:T(8,128)(2,1)} %copy.119) | copy-start | bytes 2359300
  238.8 5.4 %copy-start.23 = (bf16[2,256,768]{2,1,0:T(8,128)(2,1)S(1)}, bf16[2,256,768]{2,1,0:T(8,128)(2,1)}, u32[]{:S(2)}) copy-start(bf16[2,256,768]{2,1,0:T(8,128)(2,1)} %copy.117) | copy-start | bytes 2359300
  238.8 5.4 %copy-start.24 = (bf16[2,256,768]{2,1,0:T(8,128)(2,1)S(1)}, bf16[2,256,768]{2,1,0:T(8,128)(2,1)}, u32[]{:S(2)}) copy-start(bf16[2,256,768]{2,1,0:T(8,128)(2,1)} %copy.118) | copy-start | bytes 2359300
  251.3 9.3 %slice-start = ((s8[6291456]{0:T(1024)(128)(4,1)}), s8[2097152]{0:T(1024)(128)(4,1)S(1)}, s32[]{:S(2)}) async-start(s8[6291456]{0:T(1024)(128)(4,1)} %bitcast.217), calls=%async_computation.2 | async-start | bytes 4194304
  255.4 5.2 %slice-start.1 = ((s8[6291456]{0:T(1024)(128)(4,1)}), s8[4194304]{0:T(1024)(128)(4,1)S(1)}, s32[]{:S(2)}) async-start(s8[6291456]{0:T(1024)(128)(4,1)} %bitcast.217), calls=%async_computation.3 | async-start | bytes 8388608
  255.4 5.2 %copy-start.19 = (bf16[2,256,768]{1,2,0:T(8,128)(2,1)S(1)}, bf16[2,256,768]{1,2,0:T(8,128)(2,1)}, u32[]{:S(2)}) copy-start(bf16[2,256,768]{1,2,0:T(8,128)(2,1)} %copy.103) | copy-start | bytes 2359300
  255.4 5.2 %copy-start.26 = (bf16[2,256,768]{1,2,0:T(8,128)(2,1)S(1)}, bf16[2,256,768]{1,2,0:T(8,128)(2,1)}, u32[]{:S(2)}) copy-start(bf16[2,256,768]{1,2,0:T(8,128)(2,1)} %copy.120) | copy-start | bytes 2359300
  278.4 6.3 %copy-start.21 = (bf16[2,256,768]{2,1,0:T(8,128)(2,1)S(1)}, bf16[2,256,768]{2,1,0:T(8,128)(2,1)}, u32[]{:S(2)}) copy-start(bf16[2,256,768]{2,1,0:T(8,128)(2,1)} %copy.124) | copy-start | bytes 2359300
  392.3 9.3 %copy-start.27 = (f32[96,768]{1,0:T(8,128)S(1)}, f32[96,768]{1,0:T(8,128)}, u32[]{:S(2)}) copy-start(f32[96,768]{1,0:T(8,128)} %get-tuple-element.36) | copy-start | bytes 884740
  392.3 10.0 %copy-start.13 = (bf16[2,2,2,4,23,768]{5,4,3,2,1,0:T(8,128)(2,1)S(1)}, bf16[2,2,2,4,23,768]{5,4,3,2,1,0:T(8,128)(2,1)}, u32[]{:S(2)}) copy-start(bf16[2,2,2,4,23,768]{5,4,3,2,1,0:T(8,128)(2,1)} %get-tuple-element.37) | copy-start | bytes 3391492
  (15 other events, 41.5 us)

commit v3 on v1

--- a/solution.py
+++ b/solution.py
@@ -3,6 +3,8 @@
 import jax
 import jax.numpy as jnp
 from jax import lax
+from jax.experimental import pallas as pl
+from jax.experimental.pallas import tpu as pltpu
 from jax.sharding import PartitionSpec as P
 
 D = 768
@@ -14,6 +16,48 @@
 MASKED = -1e30
 F32 = jnp.float32
 BF16 = jnp.bfloat16
+GELU = math.sqrt(2.0 / math.pi)
+MESH = pl.DeviceIdType.MESH
+DEVICES = 32
+OWNERS = 9 * D // 256
+SHARE = (10 * D + FF) // DEVICES
+SPATIAL = 16
+TOKENS = 256
+VMEM_LIMIT = 67_000_000
+
+
+def dot(a, b):
+    return jnp.dot(a, b, preferred_element_type=F32)
+
+
+def place():
+    w, z = lax.axis_index("wide"), lax.axis_index("narrow")
+    return w // 4, (w // 2) % 2, w % 2, z
+
+
+def device_at(y, x, c, z):
+    return {"wide": (y * 2 + x) * 2 + c, "narrow": z}
+
+
+def remote(src, dst, send, recv, target):
+    return pltpu.make_async_remote_copy(
+        src_ref=src, dst_ref=dst, send_sem=send, recv_sem=recv,
+        device_id=target, device_id_type=MESH,
+    )
+
+
+class Sender:
+    def __init__(self):
+        self.copies = []
+
+    def go(self, src, dst, send, recv, target):
+        copy = remote(src, dst, send, recv, target)
+        copy.start()
+        self.copies.append(copy)
+
+    def drain(self):
+        for copy in self.copies:
+            copy.wait_send()
 
 
 def timestep_condition(step_values):
@@ -21,6 +65,926 @@
     frequency = jnp.exp(-math.log(10000.0) * jnp.arange(half_width, dtype=F32) / half_width)
     angles = step_values.astype(F32)[:, None] * frequency
     return jax.nn.silu(jnp.concatenate([jnp.cos(angles), jnp.sin(angles)], axis=-1)).astype(BF16)
+
+
+class Gather:
+    SEMAPHORES = (3, 3, 10, 10, 3, 3, 3, 3)
+
+    def __init__(self, here, sender, own, out, semaphores, local):
+        self.here, self.sender, self.own, self.out, self.local = here, sender, own, out, local
+        self.zs, self.zr, self.cs, self.cr, self.xs, self.xr, self.ys, self.yr = semaphores
+        y, x, c, z = here
+        self.sib = device_at(y, x, 1 - c, z)
+        self.xn = device_at(y, 1 - x, c, z)
+        self.yn = device_at(1 - y, x, c, z)
+
+    @staticmethod
+    def scratch(count):
+        kinds = [pltpu.SemaphoreType.DMA((count, k)) for k in Gather.SEMAPHORES]
+        return kinds + [pltpu.SemaphoreType.DMA((count,))]
+
+    def start(self, i):
+        y, x, c, z = self.here
+        mine = self.out[i].at[y, x, c, z]
+        for step in (2, 1, 3):
+            self.sender.go(
+                self.own[i], mine, self.zs.at[i, step - 1],
+                self.zr.at[i, step - 1], device_at(y, x, c, (z + step) % 4),
+            )
+        pltpu.make_async_copy(self.own[i], mine, self.local.at[i]).start()
+        self.sender.go(self.own[i], mine, self.cs.at[i, 0], self.cr.at[i, 0], self.sib)
+
+    def along(self, ref, send, recv, target):
+        self.sender.go(ref, ref, send, recv, target)
+
+    def arrived(self, ref, send, recv):
+        remote(ref, ref, send, recv, self.sib).wait_recv()
+
+    def across(self, i, k, ref):
+        self.sender.go(ref, ref, self.cs.at[i, k], self.cr.at[i, k], self.sib)
+
+    def stage1(self, i):
+        y, x, c, z = self.here
+        out = self.out[i]
+        pltpu.make_async_copy(self.own[i], out.at[y, x, c, z], self.local.at[i]).wait()
+        for step in (1, 2, 3):
+            self.arrived(out.at[y, x, c, (z + 4 - step) % 4], self.zs.at[i, step - 1], self.zr.at[i, step - 1])
+        low, high = out.at[y, x, c, pl.ds(0, 2)], out.at[y, x, c, pl.ds(2, 2)]
+        self.along(low, self.xs.at[i, 0], self.xr.at[i, 0], self.xn)
+        self.along(high, self.ys.at[i, 0], self.yr.at[i, 0], self.yn)
+        self.along(high, self.xs.at[i, 1], self.xr.at[i, 1], self.xn)
+        self.along(low, self.ys.at[i, 1], self.yr.at[i, 1], self.yn)
+        for step in (1, 2, 3):
+            self.across(i, step, out.at[y, x, c, (z + 4 - step) % 4])
+
+    def stage2(self, i):
+        y, x, c, z = self.here
+        low_x = self.out[i].at[y, 1 - x, c, pl.ds(0, 2)]
+        high_y = self.out[i].at[1 - y, x, c, pl.ds(2, 2)]
+        self.arrived(low_x, self.xs.at[i, 0], self.xr.at[i, 0])
+        self.along(low_x, self.ys.at[i, 2], self.yr.at[i, 2], self.yn)
+        self.arrived(high_y, self.ys.at[i, 0], self.yr.at[i, 0])
+        self.along(high_y, self.xs.at[i, 2], self.xr.at[i, 2], self.xn)
+        self.across(i, 4, low_x)
+        self.across(i, 5, high_y)
+
+    def stage3(self, i):
+        y, x, c, z = self.here
+        out = self.out[i]
+        arrivals = (
+            (out.at[y, 1 - x, c, pl.ds(2, 2)], self.xs.at[i, 1], self.xr.at[i, 1]),
+            (out.at[1 - y, x, c, pl.ds(0, 2)], self.ys.at[i, 1], self.yr.at[i, 1]),
+            (out.at[1 - y, 1 - x, c, pl.ds(2, 2)], self.xs.at[i, 2], self.xr.at[i, 2]),
+            (out.at[1 - y, 1 - x, c, pl.ds(0, 2)], self.ys.at[i, 2], self.yr.at[i, 2]),
+        )
+        for k, (ref, send, recv) in enumerate(arrivals):
+            self.arrived(ref, send, recv)
+            self.across(i, 6 + k, ref)
+
+    def finish(self, i):
+        y, x, c, z = self.here
+        o = 1 - c
+        out = self.out[i]
+        arrivals = [out.at[y, x, o, (z + 4 - step) % 4] for step in (0, 1, 2, 3)]
+        arrivals += [
+            out.at[y, 1 - x, o, pl.ds(0, 2)],
+            out.at[1 - y, x, o, pl.ds(2, 2)],
+            out.at[y, 1 - x, o, pl.ds(2, 2)],
+            out.at[1 - y, x, o, pl.ds(0, 2)],
+            out.at[1 - y, 1 - x, o, pl.ds(2, 2)],
+            out.at[1 - y, 1 - x, o, pl.ds(0, 2)],
+        ]
+        for k, ref in enumerate(arrivals):
+            self.arrived(ref, self.cs.at[i, k], self.cr.at[i, k])
+
+
+class Names:
+    def __init__(self, names, refs):
+        for name, ref in zip(names, refs, strict=True):
+            setattr(self, name, ref)
+
+
+def rows_of(item, step, size):
+    return pl.ds(pl.multiple_of(item * TOKENS + step * size, size), size)
+
+
+def lane_cols(start, size=128):
+    return pl.ds(pl.multiple_of(start, 128), size)
+
+
+def dot_t(a, b):
+    return lax.dot_general(a, b, (((1,), (1,)), ((), ())), preferred_element_type=F32)
+
+
+def t_dot(a, b):
+    return lax.dot_general(a, b, (((0,), (0,)), ((), ())), preferred_element_type=F32)
+
+
+def weight_block(ref, start, size):
+    cols = ref[:, :, :, :, :, pl.ds(start, size)]
+    return cols.reshape(-1, size)
+
+
+def two_heads(x, scale):
+    lane = lax.broadcasted_iota(jnp.int32, x.shape, 1)
+    x = x * jnp.asarray(scale, x.dtype)
+    zero = jnp.zeros_like(x)
+    return jnp.concatenate([jnp.where(lane < HD, x, zero), jnp.where(lane >= HD, x, zero)], axis=0)
+
+
+def pick_heads(first, second):
+    lane = lax.broadcasted_iota(jnp.int32, first.shape, 1)
+    return jnp.where(lane < HD, first, second)
+
+
+def norm_rows(v):
+    centre = v - jnp.mean(v, axis=-1, keepdims=True)
+    inverse = lax.rsqrt(jnp.mean(centre * centre, axis=-1, keepdims=True) + EPS)
+    return centre * inverse, inverse
+
+
+CHUNK = 32
+PAIRS = HEADS // 2
+TENSORS = ("qs", "ps", "qt", "pt", "up", "down")
+SETS = ("n", "r", "h", "q", "p", "c", "a")
+
+
+def save_shapes(tokens):
+    rows = 2 * tokens
+    attention = {
+        "n": ((rows, D), BF16), "r": ((rows, 1), F32), "h": ((rows, D), BF16),
+        "q": ((rows, 3 * D), BF16), "p": ((rows, 2 * PAIRS * tokens), BF16),
+        "c": ((rows, D), BF16), "a": ((rows, D), BF16),
+    }
+    out = {}
+    for k in (1, 2):
+        out.update({name + str(k): spec for name, spec in attention.items()})
+    out.update({
+        "n3": ((rows, D), BF16), "r3": ((rows, 1), F32), "h3": ((rows, D), BF16),
+        "g": ((rows, FF), BF16), "gp": ((rows, FF), BF16), "mods": ((9, 8, D), F32),
+    })
+    return out
+
+
+def norm_into(s, k, shift, scale, rows, item, v):
+    n, r = norm_rows(v)
+    getattr(s, "n" + k)[rows, :] = n.astype(BF16)
+    getattr(s, "r" + k)[rows, :] = r
+    h = n * (1.0 + s.mods[scale, item : item + 1, :]) + s.mods[shift, item : item + 1, :]
+    getattr(s, "h" + k)[rows, :] = h.astype(BF16)
+
+
+def project(s, k, weight):
+    h, q = getattr(s, "h" + k), getattr(s, "q" + k)
+    for j in range(3):
+        q[:, j * D : (j + 1) * D] = dot(h[...], weight_block(weight, j * D, D)).astype(BF16)
+
+
+def attend(s, k, bias_of, first, last):
+    q, p, c = getattr(s, "q" + k), getattr(s, "p" + k), getattr(s, "c" + k)
+
+    def body(step, _):
+        item, pair = step // PAIRS, step % PAIRS
+        rows = pl.ds(pl.multiple_of(item * TOKENS, TOKENS), TOKENS)
+        at = [lane_cols(pair * 128 + j * D) for j in range(3)]
+        scores = dot_t(two_heads(q[rows, at[0]], HD ** (-0.5)), q[rows, at[1]])
+        scores = (scores.reshape(2, TOKENS, TOKENS) + bias_of(item)).reshape(2 * TOKENS, TOKENS)
+        expanded = jnp.exp(scores - jnp.max(scores, axis=-1, keepdims=True))
+        soft = (expanded * (1.0 / jnp.sum(expanded, axis=-1, keepdims=True))).astype(BF16)
+        p[:, lane_cols(step * TOKENS, TOKENS)] = soft
+        context = dot(soft, q[rows, at[2]])
+        c[rows, at[0]] = pick_heads(context[:TOKENS], context[TOKENS:]).astype(BF16)
+        return 0
+
+    lax.fori_loop(first, last, body, 0)
+
+
+def after_attention(s, k, next_k, weight, gate, shift, scale):
+    s.acc[...] = dot(getattr(s, "c" + k)[...], weight_block(weight, 0, D))
+    for item in range(2):
+        def body(t, _):
+            rows = rows_of(item, t, CHUNK)
+            a = s.acc[rows, :]
+            v = s.x[rows, :] + s.mods[gate, item : item + 1, :] * a
+            s.x[rows, :] = v
+            getattr(s, "a" + k)[rows, :] = a.astype(BF16)
+            norm_into(s, next_k, shift, scale, rows, item, v)
+            return 0
+
+        lax.fori_loop(0, TOKENS // CHUNK, body, 0)
+
+
+def flat_bias(s):
+    s.bias[...] = jnp.zeros_like(s.bias)
+    for d in range(DEVICES):
+        y, x, c, z = d // 16, (d // 8) % 2, (d // 4) % 2, d % 4
+        piece = s.small_all[y, x, c, z].astype(F32)[2:3, :512]
+        lane = lax.broadcasted_iota(jnp.int32, piece.shape, 1)
+        piece = jnp.where(lane < SHARE, piece, 0.0)
+        start = d * SHARE
+        if start % 128:
+            piece = pltpu.roll(piece, start % 128, 1)
+        low = start // 128 * 128
+        s.bias[:, low : low + 512] = s.bias[:, low : low + 512] + piece
+
+
+def forward_kernel(names, *refs):
+    s = Names(names, refs)
+    here = place()
+    y, x, c, z = here
+    me = ((y * 2 + x) * 2 + c) * 4 + z
+    sender = Sender()
+    weights = [getattr(s, "w_" + t) for t in TENSORS]
+    own = [getattr(s, "own_" + t) for t in TENSORS]
+    gather = Gather(here, sender, own, weights, [getattr(s, f"gs{i}") for i in range(8)], s.gs8)
+    little = Gather(here, sender, [s.small], [s.small_all], [getattr(s, f"ls{i}") for i in range(8)], s.ls8)
+    saves = []
+
+    def save(*names):
+        for name in names:
+            copy = pltpu.make_async_copy(getattr(s, name), getattr(s, "out_" + name), s.save_sem.at[len(saves)])
+            copy.start()
+            saves.append(copy)
+
+    def target(k):
+        d = (me + k) % DEVICES
+        return d, {"wide": d // 4, "narrow": d % 4}
+
+    barrier = pltpu.get_barrier_semaphore()
+
+    def signal(k, _):
+        pl.semaphore_signal(barrier, inc=1, device_id=target(k)[1], device_id_type=MESH)
+        return 0
+
+    lax.fori_loop(1, DEVICES, signal, 0)
+    pl.semaphore_wait(barrier, DEVICES - 1)
+
+    def columns_copy(k):
+        d, there = target(k)
+        src = s.ada.at[:, lane_cols(d * 256, 256)]
+        return d, remote(src, s.ada_cols.at[me], s.a_send.at[k], s.a_recv.at[me], there)
+
+    little.start(0)
+
+    def send_columns(k, _):
+        d, copy = columns_copy(k)
+
+        @pl.when(d < OWNERS)
+        def _():
+            copy.start()
+
+        return 0
+
+    lax.fori_loop(1, DEVICES, send_columns, 0)
+    owner = me < OWNERS
+    mine = jnp.minimum(me, OWNERS - 1)
+    own_columns = pltpu.make_async_copy(s.ada.at[:, lane_cols(mine * 256, 256)], s.ada_cols.at[me], s.own_sem.at[0])
+    own_columns.start()
+    gather.start(0)
+    gather.start(1)
+
+    place_of = lambda n: lax.broadcasted_iota(jnp.int32, (TOKENS, TOKENS), n)
+    same_frame = place_of(0) // SPATIAL == place_of(1) // SPATIAL
+    same_place = place_of(0) % SPATIAL == place_of(1) % SPATIAL
+    for item in range(2):
+        s.space_bias[item] = jnp.where(same_frame, s.keys[item : item + 1, :], MASKED)
+    s.time_bias[...] = jnp.where(same_place, 0.0, MASKED)
+
+    little.stage1(0)
+    little.stage2(0)
+    little.stage3(0)
+    little.finish(0)
+    flat_bias(s)
+    own_columns.wait()
+
+    def modulation_copy(k):
+        d, there = target(k)
+        src = s.mod_cols.at[pl.ds(pl.multiple_of(d * 8, 8), 8)]
+        return remote(src, s.mod_all.at[me], s.m_send.at[k], s.m_recv.at[me], there)
+
+    own_mod = pltpu.make_async_copy(
+        s.mod_cols.at[pl.ds(pl.multiple_of(me * 8, 8), 8)], s.mod_all.at[mine], s.own_sem.at[1]
+    )
+
+    conditions = s.small_all[...].reshape(DEVICES * 8, D)
+    part = D // DEVICES
+    spot = lambda shape, n: lax.broadcasted_iota(jnp.int32, shape, n)
+    col = spot((D, 128), 1)
+    wanted = (spot((D, 128), 0) == me * part + col) & (col < part)
+    mine_only = dot(conditions, wanted.astype(F32).astype(BF16)).astype(BF16)
+    row, item = spot((D, DEVICES * 8), 0), spot((D, DEVICES * 8), 1)
+    slot = row % part
+    copy_of = (row // part == item // 8) & (slot // 9 == item % 8) & (slot < 18)
+    s.chosen[...] = dot(copy_of.astype(F32).astype(BF16), mine_only).astype(BF16)
+
+    @pl.when(owner)
+    def _():
+        def wait_columns(k, _):
+            d, there = target(k)
+            remote(s.ada_cols.at[d], s.ada_cols.at[d], s.a_send.at[k], s.a_recv.at[d], there).wait_recv()
+            return 0
+
+        lax.fori_loop(1, DEVICES, wait_columns, 0)
+        s.mod_cols[...] = dot(conditions, s.ada_cols[...].reshape(D, 256))
+
+        def send_modulation(k, _):
+            modulation_copy(k).start()
+            return 0
+
+        lax.fori_loop(1, DEVICES, send_modulation, 0)
+        own_mod.start()
+
+    gather.start(2)
+    gather.stage1(0)
+    gather.start(3)
+    gather.stage1(1)
+    gather.stage2(0)
+
+    @pl.when(owner)
+    def _():
+        own_mod.wait()
+
+    def wait_modulation(k, _):
+        d, there = target(k)
+
+        @pl.when(d < OWNERS)
+        def _():
+            remote(s.mod_all.at[d], s.mod_all.at[d], s.m_send.at[k], s.m_recv.at[d], there).wait_recv()
+
+        return 0
+
+    lax.fori_loop(1, DEVICES, wait_modulation, 0)
+    for j in range(9):
+        row = jnp.concatenate([s.mod_all[3 * j + i] for i in range(3)], axis=1)
+        s.mods[j] = row + s.bias[:, j * D : (j + 1) * D]
+    save("mods")
+
+    for item in range(2):
+        def first(t, _):
+            rows = rows_of(item, t, CHUNK)
+            v = s.latents[rows, :].astype(F32)
+            s.x[rows, :] = v
+            norm_into(s, "1", 0, 1, rows, item, v)
+            return 0
+
+        lax.fori_loop(0, TOKENS // CHUNK, first, 0)
+    save("n1", "r1", "h1")
+
+    def ready(i):
+        gather.finish(i)
+        save("w_" + TENSORS[i])
+
+    gather.stage2(1)
+    gather.start(4)
+    gather.stage1(2)
+    gather.stage3(0)
+    ready(0)
+    project(s, "1", s.w_qs)
+    gather.stage3(1)
+    gather.start(5)
+    gather.stage1(3)
+    gather.stage2(2)
+    space = lambda item: s.space_bias[item]
+    attend(s, "1", space, 0, 3)
+    gather.stage2(3)
+    attend(s, "1", space, 3, 6)
+    gather.stage1(4)
+    attend(s, "1", space, 6, 9)
+    gather.stage3(2)
+    attend(s, "1", space, 9, 12)
+    gather.stage3(3)
+    ready(1)
+    after_attention(s, "1", "2", s.w_ps, 2, 3, 4)
+    save("q1", "p1", "c1", "a1", "n2", "r2", "h2")
+    ready(2)
+    gather.stage2(4)
+    project(s, "2", s.w_qt)
+    gather.stage1(5)
+    time = lambda item: s.time_bias[...]
+    attend(s, "2", time, 0, 3)
+    gather.stage3(4)
+    attend(s, "2", time, 3, 6)
+    gather.stage2(5)
+    attend(s, "2", time, 6, 12)
+    ready(3)
+    after_attention(s, "2", "3", s.w_pt, 5, 6, 7)
+    save("q2", "p2", "c2", "a2", "n3", "r3", "h3")
+    ready(4)
+    for j in range(FF // D):
+        s.acc[...] = dot(s.h3[...], weight_block(s.w_up, j * D, D))
+        b_up = s.bias[:, (9 + j) * D : (10 + j) * D]
+
+        def activate(t, _):
+            rows = rows_of(0, t, CHUNK)
+            u = s.acc[rows, :] + b_up
+            square = u * u
+            th = jnp.tanh(u * (GELU + (GELU * 0.044715) * square))
+            half = 0.5 * u
+            s.g[rows, j * D : (j + 1) * D] = (half + half * th).astype(BF16)
+            slope = 0.5 + 0.5 * th + half * (1.0 - th * th) * (GELU + (3 * GELU * 0.044715) * square)
+            s.gp[rows, j * D : (j + 1) * D] = slope.astype(BF16)
+            return 0
+
+        lax.fori_loop(0, 2 * TOKENS // CHUNK, activate, 0)
+        if j == 1:
+            gather.stage3(5)
+    save("g", "gp")
+    ready(5)
+    for j in range(FF // D):
+        w = s.w_down[j // 2, j % 2].reshape(D, D)
+        part = dot(s.g[:, j * D : (j + 1) * D], w)
+        s.acc[...] = part if j == 0 else s.acc[...] + part
+    b_down = s.bias[:, (9 + FF // D) * D : (10 + FF // D) * D]
+    for item in range(2):
+        gate = s.mods[8, item : item + 1, :]
+
+        def last(t, total):
+            rows = rows_of(item, t, CHUNK)
+            m = s.acc[rows, :] + b_down
+            valid = s.valid[rows, :]
+            s.output[rows, :] = ((s.x[rows, :] + gate * m) * valid).astype(BF16)
+            d3 = s.cotangent[rows, :].astype(F32) * valid
+            return total + jnp.sum((d3 * m).reshape(CHUNK // 8, 8, D), axis=0)
+
+        total = lax.fori_loop(0, TOKENS // CHUNK, last, jnp.zeros((8, D), F32))
+        s.dga3[item : item + 1, :] = jnp.sum(total, axis=0, keepdims=True)
+
+    def drain(k, _):
+        d, copy = columns_copy(k)
+
+        @pl.when(d < OWNERS)
+        def _():
+            copy.wait_send()
+
+        @pl.when(owner)
+        def _():
+            modulation_copy(k).wait_send()
+
+        return 0
+
+    lax.fori_loop(1, DEVICES, drain, 0)
+    sender.drain()
+    for copy in saves:
+        copy.wait()
+
+
+def run_forward(small, ada, shards, latents, cotangent, keys, valid):
+    vmem, any_space = pl.BlockSpec(memory_space=pltpu.VMEM), pl.BlockSpec(memory_space=pl.ANY)
+    saved = save_shapes(TOKENS)
+    weights = {"w_" + t: ((2, 2, 2, 4) + sh.shape, BF16) for t, sh in zip(TENSORS, shards)}
+    kept = {**saved, **weights}
+    rows = 2 * TOKENS
+    ins = ["small", "ada"] + ["own_" + t for t in TENSORS] + ["latents", "cotangent", "keys", "valid"]
+    outs = ["output", "dga3", "chosen"] + ["out_" + name for name in kept]
+    dma = pltpu.SemaphoreType.DMA
+    scratch = {name: pltpu.VMEM(*spec) for name, spec in kept.items()}
+    scratch |= {
+        "small_all": pltpu.VMEM((2, 2, 2, 4) + small.shape, BF16),
+        "ada_cols": pltpu.VMEM((DEVICES, ada.shape[0], 256), BF16),
+        "mod_cols": pltpu.VMEM((DEVICES * 8, 256), F32),
+        "mod_all": pltpu.VMEM((OWNERS, 8, 256), F32),
+        "bias": pltpu.VMEM((1, DEVICES * SHARE + 512), F32),
+        "x": pltpu.VMEM((rows, D), F32),
+        "acc": pltpu.VMEM((rows, D), F32),
+        "space_bias": pltpu.VMEM((2, TOKENS, TOKENS), F32),
+        "time_bias": pltpu.VMEM((TOKENS, TOKENS), F32),
+        "save_sem": dma((len(kept),)),
+        "a_send": dma((DEVICES,)), "a_recv": dma((DEVICES,)),
+        "m_send": dma((DEVICES,)), "m_recv": dma((DEVICES,)), "own_sem": dma((2,)),
+    }
+    scratch |= {f"gs{i}": kind for i, kind in enumerate(Gather.scratch(len(shards)))}
+    scratch |= {f"ls{i}": kind for i, kind in enumerate(Gather.scratch(1))}
+    names = ins + outs + list(scratch)
+    results = pl.pallas_call(
+        lambda *refs: forward_kernel(names, *refs),
+        out_shape=(jax.ShapeDtypeStruct((rows, D), BF16), jax.ShapeDtypeStruct((2, D), F32), jax.ShapeDtypeStruct((D, 128), BF16))
+        + tuple(jax.ShapeDtypeStruct(*spec) for spec in kept.values()),
+        in_specs=[vmem] * len(ins),
+        out_specs=(vmem,) * 3 + (any_space,) * len(kept),
+        scratch_shapes=list(scratch.values()),
+        compiler_params=pltpu.CompilerParams(
+            collective_id=1, has_side_effects=True, vmem_limit_bytes=VMEM_LIMIT
+        ),
+        name="forward",
+    )(small, ada, *shards, latents, cotangent, keys, valid)
+    return results[0], results[1], results[2], dict(zip(kept, results[3:]))
+
+
+class Scatter:
+    SEMAPHORES = ((), (), (2,), (2,), (2,), (2,), (3,), (3,))
+    LEADING = ((2, 2, 4), (2, 2), (2, 2), (2,), (2,), (3,))
+
+    def __init__(self, here, part, out, buffers, semaphores):
+        self.here, self.part, self.out = here, part, out
+        self.r0, self.r1a, self.r1b, self.r2a, self.r2b, self.r3 = buffers
+        self.cs, self.cr, self.s1, self.v1, self.s2, self.v2, self.s3, self.v3 = semaphores
+        y, x, c, z = here
+        self.sib = device_at(y, x, 1 - c, z)
+        self.xn = device_at(y, 1 - x, c, z)
+        self.yn = device_at(1 - y, x, c, z)
+        self.copies = [[] for _ in part]
+
+    def hop(self, i, stage, k):
+        y, x, c, z = self.here
+        part = self.part[i]
+        if stage == 0:
+            return (part.at[:, :, 1 - c], self.r0[i], self.cs.at[i], self.cr.at[i], self.sib)
+        if stage == 1:
+            if k == 0:
+                return (part.at[1 - y, :, c, pl.ds(0, 2)], self.r1a[i], self.s1.at[i, 0], self.v1.at[i, 0], self.yn)
+            return (part.at[:, 1 - x, c, pl.ds(2, 2)], self.r1b[i], self.s1.at[i, 1], self.v1.at[i, 1], self.xn)
+        if stage == 2:
+            if k == 0:
+                return (part.at[y, 1 - x, c, pl.ds(0, 2)], self.r2a[i], self.s2.at[i, 0], self.v2.at[i, 0], self.xn)
+            return (part.at[1 - y, x, c, pl.ds(2, 2)], self.r2b[i], self.s2.at[i, 1], self.v2.at[i, 1], self.yn)
+        there = (z + k + 1) % 4
+        return (part.at[y, x, c, there], self.r3[i].at[k], self.s3.at[i, k], self.v3.at[i, k], device_at(y, x, c, there))
+
+    def send(self, i, stage, k):
+        copy = remote(*self.hop(i, stage, k))
+        copy.start()
+        self.copies[i].append(copy)
+
+    def wait(self, i, stage, k):
+        remote(*self.hop(i, stage, k)).wait_recv()
+
+    def drain(self, i):
+        for copy in self.copies[i]:
+            copy.wait_send()
+        self.copies[i] = []
+
+    def start(self, i):
+        self.send(i, 0, 0)
+
+    def stage1(self, i):
+        c = self.here[2]
+        part, r0 = self.part[i], self.r0[i]
+        self.wait(i, 0, 0)
+
+        def add(k, _):
+            a, b, q = k // 8, (k // 4) % 2, k % 4
+            part[a, b, c, q] = part[a, b, c, q] + r0[a, b, q]
+            return 0
+
+        lax.fori_loop(0, 16, add, 0)
+        self.send(i, 1, 0)
+        self.send(i, 1, 1)
+
+    def stage2(self, i):
+        y, x, c, z = self.here
+        part, r1a, r1b = self.part[i], self.r1a[i], self.r1b[i]
+        self.wait(i, 1, 0)
+        self.wait(i, 1, 1)
+
+        def add(k, _):
+            a, q = k // 2, k % 2
+            part[y, a, c, q] = part[y, a, c, q] + r1a[a, q]
+            part[a, x, c, q + 2] = part[a, x, c, q + 2] + r1b[a, q]
+            return 0
+
+        lax.fori_loop(0, 4, add, 0)
+        self.send(i, 2, 0)
+        self.send(i, 2, 1)
+
+    def stage3(self, i):
+        y, x, c, z = self.here
+        part = self.part[i]
+        self.wait(i, 2, 0)
+        self.wait(i, 2, 1)
+        for q in range(2):
+            part[y, x, c, q] = part[y, x, c, q] + self.r2a[i][q]
+            part[y, x, c, q + 2] = part[y, x, c, q + 2] + self.r2b[i][q]
+        for k in (1, 0, 2):
+            self.send(i, 3, k)
+
+    def stage4(self, i):
+        y, x, c, z = self.here
+        for k in range(3):
+            self.wait(i, 3, k)
+        part, r3 = self.part[i], self.r3[i]
+        flatten_into(
+            self.out[i],
+            (part[y, x, c, z].astype(F32) + r3[0].astype(F32)) + (r3[1].astype(F32) + r3[2].astype(F32)),
+            0,
+            part.shape[-1] // 128,
+        )
+
+
+def flatten_into(out, value, start, stride):
+    rows, size = value.shape
+    for k in range(size // 128):
+        out[pl.ds(start + k, rows, stride=stride), :] = value[:, k * 128 : (k + 1) * 128]
+
+
+GRADS = ("down", "up", "pt", "qt", "ps", "qs")
+WIDTHS = {"down": D, "up": FF, "pt": D, "qt": 3 * D, "ps": D, "qs": 3 * D}
+BLOCKS = [("down", j) for j in range(4)] + [("up", j) for j in range(4)]
+BLOCKS += [("pt", 0)] + [("qt", j) for j in range(3)] + [("ps", 0)] + [("qs", j) for j in range(3)]
+SLOTS = 4
+
+
+def attend_back(s, q, p, c_grad, first, last):
+    def body(step, _):
+        item, pair = step // PAIRS, step % PAIRS
+        rows = pl.ds(pl.multiple_of(item * TOKENS, TOKENS), TOKENS)
+        at = [lane_cols(pair * 128 + j * D) for j in range(3)]
+        soft = p[:, lane_cols(step * TOKENS, TOKENS)]
+        dc = c_grad[rows, at[0]]
+        queries, keys, values = (q[rows, where] for where in at)
+        v_grad = pick_heads(t_dot(soft[:TOKENS], dc), t_dot(soft[TOKENS:], dc))
+        soft_grad = dot_t(two_heads(dc, 1.0), values)
+        wide = soft.astype(F32)
+        product = soft_grad * wide
+        score = (product - wide * jnp.sum(product, axis=-1, keepdims=True)).astype(BF16)
+        q_both = dot(score, keys)
+        q_grad = pick_heads(q_both[:TOKENS], q_both[TOKENS:]) * HD ** (-0.5)
+        k_grad = pick_heads(t_dot(score[:TOKENS], queries), t_dot(score[TOKENS:], queries)) * HD ** (-0.5)
+        q[rows, at[0]] = q_grad.astype(BF16)
+        q[rows, at[1]] = k_grad.astype(BF16)
+        q[rows, at[2]] = v_grad.astype(BF16)
+        return 0
+
+    lax.fori_loop(first, last, body, 0)
+
+
+def backward_kernel(names, *refs):
+    s = Names(names, refs)
+    here = place()
+    y, x, c, z = here
+    me = ((y * 2 + x) * 2 + c) * 4 + z
+    loads = {}
+
+    def fetch(name, src, dst, k):
+        loads[name] = pltpu.make_async_copy(src, dst, s.load_sem.at[k])
+        loads[name].start()
+
+    def have(*wanted):
+        for name in wanted:
+            loads.pop(name).wait()
+
+    def fetch_block(k):
+        tensor, j = BLOCKS[k]
+        src = getattr(s, "w_" + tensor)
+        src = src.at[j] if tensor == "down" else src.at[:, :, pl.ds(j * D, D)]
+        fetch(("w", k), src, s.blocks.at[k % SLOTS], 16 + k % SLOTS)
+
+    def block(k):
+        have(("w", k))
+        return s.blocks[k % SLOTS].reshape(D, D)
+
+    def used(k):
+        if k + SLOTS < len(BLOCKS):
+            fetch_block(k + SLOTS)
+
+    fetch("g", s.in_g, s.g, 0)
+    fetch("mods", s.in_mods, s.mods, 1)
+    fetch_block(0)
+    fetch_block(1)
+    fetch("gp", s.in_gp, s.gp, 2)
+    fetch("h3", s.in_h3, s.h3, 3)
+    fetch_block(2)
+    fetch_block(3)
+    fetch("n3", s.in_n3, s.n3, 4)
+    fetch("r3", s.in_r3, s.r3, 5)
+
+    def fetch_rest(k):
+        for i, (name, dst) in enumerate((("a", s.a), ("c", s.c), ("h", s.h), ("n", s.n), ("r", s.r))):
+            fetch(name, getattr(s, f"in_{name}{k}"), dst, 6 + i)
+
+    fetch_rest(2)
+
+    parts = [s.b0, s.b1]
+    parts += [s.b2.at[:, :, :, :, :, pl.ds(0, D)], s.b2.at[:, :, :, :, :, pl.ds(D, 3 * D)]]
+    parts += [s.b3, s.b1.at[:, :, :, :, :, pl.ds(0, 3 * D)]]
+    outs = [getattr(s, "grad_" + t) for t in GRADS]
+    buffers = [[getattr(s, f"r{k}_{t}") for t in GRADS] for k in range(6)]
+    scatter = Scatter(here, parts, outs, buffers, [getattr(s, f"ss{k}") for k in range(8)])
+    sender = Sender()
+    little = Gather(here, sender, [s.small], [s.small_all], [getattr(s, f"ls{i}") for i in range(8)], s.ls8)
+
+    barrier = pltpu.get_barrier_semaphore()
+    partners = [device_at(y, x, 1 - c, z), device_at(y, 1 - x, c, z), device_at(1 - y, x, c, z)]
+    partners += [device_at(y, x, c, (z + step) % 4) for step in (1, 2, 3)]
+    for partner in partners:
+        pl.semaphore_signal(barrier, inc=1, device_id=partner, device_id_type=MESH)
+    pl.semaphore_wait(barrier, 6)
+
+    s.rows[...] = jnp.zeros_like(s.rows)
+    ones = jnp.ones((8, 2 * TOKENS), BF16)
+    have("mods")
+    for item in range(2):
+        gate = s.mods[8, item : item + 1, :]
+
+        def first(t, _):
+            rows = rows_of(item, t, CHUNK)
+            d3 = s.cotangent[rows, :].astype(F32) * s.valid[rows, :]
+            s.d[rows, :] = d3
+            s.dm[rows, :] = (gate * d3).astype(BF16)
+            return 0
+
+        lax.fori_loop(0, TOKENS // CHUNK, first, 0)
+        s.rows[9 * item + 8 : 9 * item + 9, :] = s.dga3[item : item + 1, :]
+    s.rows[22:23, :] = dot(ones, s.dm[...])[:1]
+
+    have("g")
+    for j in range(4):
+        grad = t_dot(s.g[:, j * D : (j + 1) * D], s.dm[...]).astype(BF16)
+        s.b0[j // 2, j % 2] = grad.reshape(2, 4, 4 * D // DEVICES, D)
+    scatter.start(0)
+    fetch("p", s.in_p2, s.g, 0)
+
+    have("gp", "h3")
+    for j in range(4):
+        cols = slice(j * D, (j + 1) * D)
+        s.acc[...] = dot_t(s.dm[...], block(j))
+        used(j)
+
+        def slope(t, _):
+            rows = rows_of(0, t, CHUNK)
+            s.gp[rows, cols] = (s.acc[rows, :] * s.gp[rows, cols].astype(F32)).astype(BF16)
+            return 0
+
+        lax.fori_loop(0, 2 * TOKENS // CHUNK, slope, 0)
+        s.rows[18 + j : 19 + j, :] = dot(ones, s.gp[:, cols])[:1]
+        if j == 1:
+            scatter.stage1(0)
+    for j in range(4):
+        cols = slice(j * D, (j + 1) * D)
+        grad = t_dot(s.h3[...], s.gp[:, cols]).astype(BF16)
+        s.b1[:, :, :, :, :, cols] = grad.reshape(2, 2, 2, 4, D // DEVICES, D)
+    scatter.start(1)
+
+    def back_through(first_block, source, count):
+        for j in range(count):
+            part = dot_t(source[:, j * D : (j + 1) * D], block(first_block + j))
+            used(first_block + j)
+            s.acc[...] = part if j == 0 else s.acc[...] + part
+
+    back_through(4, s.gp, 4)
+    fetch("q", s.in_q2, s.gp.at[:, pl.ds(0, 3 * D)], 2)
+    scatter.stage1(1)
+
+    def norm_back(n_ref, r_ref, base, a_ref, gate_row):
+        for item in range(2):
+            scale = 1.0 + s.mods[base + 1, item : item + 1, :]
+            gate = None if gate_row is None else s.mods[gate_row, item : item + 1, :]
+
+            def body(t, totals):
+                rows = rows_of(item, t, CHUNK)
+                dh, n = s.acc[rows, :], n_ref[rows, :].astype(F32)
+                g = dh * scale
+                dhn = dh * n
+                mean_g = jnp.mean(g, axis=-1, keepdims=True)
+                mean_gn = jnp.mean(g * n, axis=-1, keepdims=True)
+                d = s.d[rows, :] + r_ref[rows, :] * (g - mean_g - n * mean_gn)
+                s.d[rows, :] = d
+                fold = lambda v: jnp.sum(v.reshape(CHUNK // 8, 8, D), axis=0)
+                new = [totals[0] + fold(dh), totals[1] + fold(dhn)]
+                if gate is not None:
+                    s.dm[rows, :] = (gate * d).astype(BF16)
+                    new.append(totals[2] + fold(d * a_ref[rows, :].astype(F32)))
+                return tuple(new)
+
+            count = 2 if gate is None else 3
+            totals = lax.fori_loop(0, TOKENS // CHUNK, body, (jnp.zeros((8, D), F32),) * count)
+            for where, total in zip((base, base + 1, base - 1), totals):
+                row = 9 * item + where
+                s.rows[row : row + 1, :] = jnp.sum(total, axis=0, keepdims=True)
+
+    have("n3", "r3", "a")
+    norm_back(s.n3, s.r3, 6, s.a, 5)
+    have("c")
+    s.b2[:, :, :, :, :, :D] = t_dot(s.c[...], s.dm[...]).astype(BF16).reshape(2, 2, 2, 4, D // DEVICES, D)
+    scatter.start(2)
+    s.dc[...] = dot_t(s.dm[...], block(8)).astype(BF16)
+    used(8)
+    scatter.stage2(0)
+    have("q", "p")
+    attend_back(s, s.gp, s.g, s.dc, 0, 4)
+    scatter.stage1(2)
+    attend_back(s, s.gp, s.g, s.dc, 4, 8)
+    scatter.stage3(0)
+    attend_back(s, s.gp, s.g, s.dc, 8, 12)
+    fetch("p", s.in_p1, s.g, 0)
+    have("h")
+    for j in range(3):
+        cols = slice(D + j * D, 2 * D + j * D)
+        grad = t_dot(s.h[...], s.gp[:, j * D : (j + 1) * D]).astype(BF16)
+        s.b2[:, :, :, :, :, cols] = grad.reshape(2, 2, 2, 4, D // DEVICES, D)
+    scatter.start(3)
+    scatter.stage2(1)
+    back_through(9, s.gp, 3)
+    scatter.stage2(2)
+    scatter.stage1(3)
+    fetch("q", s.in_q1, s.gp.at[:, pl.ds(0, 3 * D)], 2)
+    have("n", "r")
+    fetch("a", s.in_a1, s.a, 6)
+    fetch("c", s.in_c1, s.c, 7)
+    fetch("h", s.in_h1, s.h, 8)
+    have("a")
+    norm_back(s.n, s.r, 3, s.a, 2)
+    fetch("n", s.in_n1, s.n, 9)
+    fetch("r", s.in_r1, s.r, 10)
+    scatter.stage3(1)
+    have("c")
+    s.b3[...] = t_dot(s.c[...], s.dm[...]).astype(BF16).reshape(2, 2, 2, 4, D // DEVICES, D)
+    scatter.start(4)
+    s.dc[...] = dot_t(s.dm[...], block(12)).astype(BF16)
+    used(12)
+    scatter.stage4(0)
+    scatter.stage3(2)
+    have("q", "p")
+    attend_back(s, s.gp, s.g, s.dc, 0, 4)
+    scatter.stage1(4)
+    scatter.stage2(3)
+    attend_back(s, s.gp, s.g, s.dc, 4, 8)
+    scatter.stage4(1)
+    attend_back(s, s.gp, s.g, s.dc, 8, 12)
+    scatter.stage4(2)
+    scatter.stage3(3)
+    scatter.drain(1)
+    have("h")
+    for j in range(3):
+        cols = slice(j * D, (j + 1) * D)
+        grad = t_dot(s.h[...], s.gp[:, cols]).astype(BF16)
+        s.b1[:, :, :, :, :, cols] = grad.reshape(2, 2, 2, 4, D // DEVICES, D)
+    scatter.start(5)
+    scatter.stage2(4)
+    back_through(13, s.gp, 3)
+    scatter.stage1(5)
+    have("n", "r")
+    norm_back(s.n, s.r, 0, None, None)
+    s.small[...] = s.rows[...].astype(BF16)
+    little.start(0)
+    scatter.stage3(4)
+    little.stage1(0)
+    scatter.stage4(3)
+    little.stage2(0)
+    scatter.stage4(4)
+    little.stage3(0)
+    scatter.stage2(5)
+    little.finish(0)
+
+    gathered = s.small_all[...].reshape(D, D)
+    slot = lax.broadcasted_iota(jnp.int32, (D, 128), 0) % (D // DEVICES)
+    for j in range(9):
+        chosen = jnp.where((slot == j) | (slot == j + 9), s.chosen[...], jnp.zeros((D, 128), BF16))
+        grad = t_dot(chosen, gathered)[: D // DEVICES]
+        flatten_into(s.grad_ada, grad, j * (D // 128), 9 * D // 128)
+        if j == 5:
+            scatter.stage3(5)
+    row = lax.broadcasted_iota(jnp.int32, (16, D), 0)
+    slot = lax.broadcasted_iota(jnp.int32, (16, D), 1) % (D // DEVICES)
+    take = ((row < 9) & ((slot == row) | (slot == row + 9))) | ((row >= 9) & (slot == row + 9))
+    s.grad_bias[...] = dot(take.astype(F32).astype(BF16), gathered)
+    scatter.stage4(5)
+    for i in range(len(GRADS)):
+        scatter.drain(i)
+    sender.drain()
+
+
+def run_backward(cotangent, valid, dga3, chosen, kept):
+    vmem, any_space = pl.BlockSpec(memory_space=pltpu.VMEM), pl.BlockSpec(memory_space=pl.ANY)
+    rows, part = 2 * TOKENS, D // DEVICES
+    ins = {"cotangent": cotangent, "valid": valid, "dga3": dga3, "chosen": chosen}
+    fetched = {"in_" + name: kept[name] for name in save_shapes(TOKENS)}
+    for t in GRADS:
+        shape = (4, DEVICES, part, D) if t == "down" else (DEVICES, part, WIDTHS[t])
+        fetched["w_" + t] = kept["w_" + t].reshape(shape)
+    ins |= fetched
+    block_of = {t: (4 * part, D) if t == "down" else (part, WIDTHS[t]) for t in GRADS}
+    outs = {"grad_" + t: (DEVICES * part * WIDTHS[t] * (4 if t == "down" else 1) // DEVICES // 128, 128) for t in GRADS}
+    outs |= {"grad_ada": (part * 9 * D // 128, 128), "grad_bias": (16, D), "d": (rows, D)}
+    dma = pltpu.SemaphoreType.DMA
+    big = lambda *block: pltpu.VMEM((2, 2, 2, 4) + block, BF16)
+    scratch = {
+        "b0": big(4 * part, D), "b1": big(part, FF), "b2": big(part, FF), "b3": big(part, D),
+        "blocks": pltpu.VMEM((SLOTS, DEVICES, part, D), BF16),
+        "g": pltpu.VMEM((rows, FF), BF16), "gp": pltpu.VMEM((rows, FF), BF16),
+        "acc": pltpu.VMEM((rows, D), F32),
+        "mods": pltpu.VMEM((9, 8, D), F32), "rows": pltpu.VMEM((24, D), F32),
+        "small": pltpu.VMEM((24, D), BF16), "small_all": big(24, D),
+        "r3": pltpu.VMEM((rows, 1), F32), "r": pltpu.VMEM((rows, 1), F32),
+        "load_sem": dma((16 + SLOTS,)),
+    }
+    scratch |= {name: pltpu.VMEM((rows, D), BF16) for name in ("dm", "dc", "h3", "n3", "a", "c", "h", "n")}
+    for k, lead in enumerate(Scatter.LEADING):
+        scratch |= {f"r{k}_{t}": pltpu.VMEM(lead + block_of[t], BF16) for t in GRADS}
+    scratch |= {f"ss{k}": dma((len(GRADS),) + extra) for k, extra in enumerate(Scatter.SEMAPHORES)}
+    scratch |= {f"ls{i}": kind for i, kind in enumerate(Gather.scratch(1))}
+    names = list(ins) + list(outs) + list(scratch)
+    results = pl.pallas_call(
+        lambda *refs: backward_kernel(names, *refs),
+        out_shape=tuple(jax.ShapeDtypeStruct(shape, F32) for shape in outs.values()),
+        in_specs=[vmem] * 4 + [any_space] * len(fetched),
+        out_specs=(vmem,) * len(outs),
+        scratch_shapes=list(scratch.values()),
+        compiler_params=pltpu.CompilerParams(
+            collective_id=2, has_side_effects=True, vmem_limit_bytes=VMEM_LIMIT
+        ),
+        name="backward",
+    )(*ins.values())
+    return dict(zip(outs, results))
 
 
 def norm_parts(rows):
@@ -39,10 +1003,6 @@
         - normed * jnp.mean(pulled * normed, axis=-1, keepdims=True)
     )
     return back, shift_grad, scale_grad
-
-
-def dot(a, b):
-    return jnp.dot(a, b, preferred_element_type=F32)
 
 
 def heads(x):
@@ -78,30 +1038,47 @@
     return low_grad, qkv_grad, proj_grad
 
 
-def per_device(latents, buckets, step_ids, qs, ps, qt, pt, up, down, ada, biases, cotangent):
+def gather_plain(shards):
+    return tuple(lax.all_gather(s, AXES, axis=0) for s in shards)
+
+
+def scatter_plain(parts, small):
+    devices = lax.axis_size(AXES)
+    sums = tuple(
+        lax.psum_scatter(p.reshape((devices,) + p.shape[-2:]), AXES, scatter_dimension=0, tiled=True)[
+            0
+        ].astype(F32)
+        for p in parts
+    )
+    return sums + (lax.all_gather(small, AXES, axis=0),)
+
+
+def per_device_plain(latents, buckets, step_ids, qs, ps, qt, pt, up, down, ada, biases, cotangent):
     devices = lax.axis_size(AXES)
     micro = latents.shape[0]
     frames, spatial = latents.shape[2], latents.shape[3]
     tokens = frames * spatial
     rows = D // devices
 
-    steps = lax.all_gather(step_ids[:, 0], AXES, axis=0, tiled=True)
-    condition = timestep_condition(steps)
+    gather, scatter = gather_plain, scatter_plain
+
     ada_columns = lax.all_to_all(
         ada.reshape(rows, 9 * D), AXES, split_axis=1, concat_axis=0, tiled=True
     )
+    own_bias = jnp.pad(biases, (0, D - biases.shape[0]))[None]
+    small = jnp.concatenate([timestep_condition(step_ids[:, 0]), own_bias], axis=0)
+    shards = [small] + [w.reshape(rows, -1) for w in (qs, ps, qt, pt, up)] + [down.reshape(-1, D)]
+    small, *gathered = gather(shards)
+    w_qs, w_ps, w_qt, w_pt, w_up = (w.reshape(D, -1) for w in gathered[:5])
+    w_down = gathered[5].reshape(-1, D)
+    small = small.reshape(devices, micro + 1, D)
+    condition = small[:, :micro].reshape(devices * micro, D)
+    bias = small[:, micro, : biases.shape[0]].reshape(-1).astype(F32)
     modulation = lax.all_to_all(
         dot(condition, ada_columns), AXES, split_axis=0, concat_axis=1, tiled=True
     )
-    bias = lax.all_gather(biases, AXES, axis=0, tiled=True).astype(F32)
     modulation = (modulation + bias[: 9 * D]).reshape(micro, 9, 1, D)
     b_up, b_down = bias[9 * D : 9 * D + FF], bias[9 * D + FF :]
-
-    wide_shard = jnp.concatenate([w.reshape(rows, -1) for w in (qs, ps, qt, pt, up)], axis=1)
-    wide = lax.all_gather(wide_shard, AXES, axis=0, tiled=True)
-    w_down = lax.all_gather(down.reshape(-1, D), AXES, axis=0, tiled=True)
-    cuts = [3 * D, 4 * D, 7 * D, 8 * D]
-    w_qs, w_ps, w_qt, w_pt, w_up = jnp.split(wide, cuts, axis=1)
 
     positions = jnp.arange(tokens)
     frame, place = positions // spatial, positions % spatial
@@ -154,10 +1131,18 @@
     dv, dsh1, dsc1 = norm_back(dh1, n1, r1, sc1)
     latents_grad = d1 + dv
 
-    dmod = jnp.concatenate([dsh1, dsc1, dga1, dsh2, dsc2, dga2, dsh3, dsc3, dga3], axis=-1)
-    small = jnp.concatenate([dmod.reshape(1, -1), db_up[None], db_down[None]], axis=-1)
-    small = lax.all_gather(small.astype(BF16), AXES, axis=0, tiled=True)
-    dmod_all = small[:, : micro * 9 * D].reshape(devices * micro, 9 * D)
+    dmod = jnp.stack([dsh1, dsc1, dga1, dsh2, dsc2, dga2, dsh3, dsc3, dga3], axis=1)
+    small = jnp.concatenate(
+        [dmod.reshape(micro * 9, D), db_up.reshape(-1, D), db_down.reshape(-1, D)], axis=0
+    ).astype(BF16)
+    parts = [
+        part.astype(BF16).reshape(tuple(gathered[i].shape))
+        for i, part in ((5, dw_down), (4, dw_up), (3, dw_pt), (2, dw_qt), (1, dw_ps), (0, dw_qs))
+    ]
+    ddown, dup, dpt, dqt, dps, dqs, small = scatter(parts, small)
+    flat = tuple(part.reshape(-1) for part in (dqs, dps, dqt, dpt, dup))
+    small = small.reshape(devices, -1, D)
+    dmod_all = small[:, : micro * 9].reshape(devices * micro, 9 * D)
     me = lax.axis_index(AXES)
     my_condition = lax.dynamic_slice_in_dim(condition, me * rows, rows, axis=1)
     dw_ada = lax.dot_general(
@@ -166,15 +1151,11 @@
     db = jnp.concatenate(
         [
             jnp.sum(dmod_all.astype(F32), axis=0),
-            jnp.sum(small[:, micro * 9 * D :].astype(F32), axis=0),
+            jnp.sum(small[:, micro * 9 :].astype(F32), axis=0).reshape(-1),
         ]
     )
     db = lax.dynamic_slice_in_dim(db, me * biases.shape[0], biases.shape[0])
 
-    dwide = jnp.concatenate([w.astype(BF16) for w in (dw_qs, dw_ps, dw_qt, dw_pt, dw_up)], axis=1)
-    dwide = lax.psum_scatter(dwide, AXES, scatter_dimension=0, tiled=True).astype(F32)
-    ddown = lax.psum_scatter(dw_down.astype(BF16), AXES, scatter_dimension=0, tiled=True).astype(F32)
-    flat = tuple(part.reshape(-1) for part in jnp.split(dwide, cuts, axis=1))
     shape = latents.shape
     return (
         output.reshape(shape),
@@ -186,11 +1167,41 @@
     )
 
 
+def per_device(latents, buckets, step_ids, qs, ps, qt, pt, up, down, ada, biases, cotangent):
+    devices = lax.axis_size(AXES)
+    part = D // devices
+    rows = 2 * TOKENS
+    own_bias = jnp.pad(biases, (0, D - biases.shape[0]))[None]
+    conditions = timestep_condition(step_ids[:, 0])
+    small = jnp.concatenate([conditions, own_bias, jnp.zeros((5, D), BF16)], axis=0)
+    bucket = buckets[:, 0]
+    length = jnp.where(bucket == 0, SPATIAL, jnp.where(bucket == 1, SPATIAL // 2, SPATIAL // 8))
+    valid = (jnp.arange(TOKENS) % SPATIAL)[None] < length[:, None]
+    keys = jnp.where(valid, 0.0, MASKED).astype(F32)
+    valid = valid.astype(F32).reshape(rows, 1)
+    shards = [w.reshape(part, -1) for w in (qs, ps, qt, pt, up)] + [down.reshape(-1, D)]
+    tokens = latents.reshape(rows, D)
+    grads_in = cotangent.reshape(rows, D)
+    output, dga3, chosen, kept = run_forward(
+        small, ada.reshape(part, -1), shards, tokens, grads_in, keys, valid
+    )
+    grads = run_backward(grads_in, valid, dga3, chosen, kept)
+    me = lax.axis_index(AXES)
+    bias_grad = grads["grad_bias"][:14].reshape(-1)
+    return (
+        output.reshape(latents.shape),
+        grads["d"].reshape(latents.shape),
+        *(grads["grad_" + t].reshape(-1) for t in ("qs", "ps", "qt", "pt", "up", "down", "ada")),
+        lax.dynamic_slice_in_dim(bias_grad, me * SHARE, SHARE),
+    )
+
+
 def solution(mesh):
     items = P(None, AXES, None, None, None)
     flat = P(AXES)
+    known = mesh.shape["wide"] == 8 and mesh.shape["narrow"] == 4
     return jax.shard_map(
-        per_device,
+        per_device if known else per_device_plain,
         mesh=mesh,
         in_specs=(items, P(None, AXES), P(None, AXES)) + (flat,) * 8 + (items,),
         out_specs=(items, items) + (flat,) * 8,

time: 645 us -> 281 us (0.44)
  waiting for transfers between devices: 302 us -> 0 us
  Pallas kernels: 0 us -> 249 us
  matrix products: 141 us -> 0 us
  blocking collectives: 86.5 us -> 0 us
  local copies, waits for them, and re-layouts: 62.7 us -> 24.7 us
  other arithmetic: 18.9 us -> 2.87 us
  between operations: 15.5 us -> 0.96 us
  starting transfers between devices: 11.9 us -> 0 us
    reduce_scatter x2 -> x0, waiting for transfers between devices: 273 us -> none  [the longest x1 166 us: per_device(): lax.psum_scatter(dwide, AXES, scatter_dimension=0, tiled=True).astype(F32)]
    pallas_call x0 -> x2, Pallas kernels: none -> 249 us  [the longest x1 125 us: run_backward(): pl.pallas_call(lambda *refs: backward_kernel(names, *refs), out_shape=tup...]
    dot_general x30 -> x0, matrix products: 130 us -> none  [the longest x7 28 us: dot(): return jnp.dot(a, b, preferred_element_type=F32)]
    unnamed x2 -> x0, blocking collectives: 86.5 us -> none
    all_gather x3 -> x0, waiting for transfers between devices: 29.1 us -> none  [the longest x1 12.8 us: per_device(): small = lax.all_gather(small.astype(BF16), AXES, axis=0, tiled=True)]
    split x10 -> x0, local copies, waits for them, and re-layouts: 14 us -> none  [the longest x8 12.2 us: attention(): q, k, v = (heads(part) for part in jnp.split(packed, 3, axis=-1))]
    all_to_all x2 -> x0, starting transfers between devices: 11.7 us -> none  [the longest x1 7.33 us: per_device(): lax.all_to_all(ada.reshape(rows, 9 * D), AXES, split_axis=1, concat_axis=...]
    reshape x19 -> x8, local copies, waits for them, and re-layouts: 24.1 us -> 12.6 us  [the longest x5 7.89 us: per_device(): w.reshape(part, -1)]
  transfers between devices with their start and end apart: 7 -> 0, of which waited for: 5 -> 0; matrix products, arithmetic and copies ran while one was open for 17% -> 0% of each run, Pallas kernels for 0% -> 0%
where the time goes in v3:
time: 281 us; the launch traced here: 278 us
  Pallas kernels  249 us (89%)
  local copies, waits for them, and re-layouts  24.7 us (9%)
  other arithmetic  2.87 us (1%)
    pallas_call x1, Pallas kernels, run_backward(): pl.pallas_call(lambda *refs: backward_kernel(names, *refs), out_shape=tup...  125 us
    pallas_call x1, Pallas kernels, run_forward(): pl.pallas_call(lambda *refs: forward_kernel(names, *refs), out_shape=(jax...  124 us
    unnamed x25, local copies, waits for them, and re-layouts  10.7 us
    reshape x5, local copies, waits for them, and re-layouts, per_device(): w.reshape(part, -1)  7.89 us

profile of v3, /device:TPU:0, one launch (start us, length us, event | category | flops | bytes accessed | tf_op | source)
XLA Modules:
  0.0 277.9 jit_solution(16008067472973048424)
XLA Ops:
  0.6 0.7 pad.4
  1.3 0.7 convert_bitcast_fusion
  2.0 0.1 multiply_cosine_fusion
  2.2 0.1 pad.7.clone
  2.3 0.7 maximum_maximum_fusion.refs_0_
  2.9 2.1 reshape.137.refs_1_
  5.0 1.7 reshape.138.refs_2_
  6.7 1.4 reshape.139.refs_3_
  8.1 1.7 reshape.140.refs_4_
  9.8 1.4 reshape.141.refs_5_
  11.3 1.6 reshape.142.refs_6_
  12.9 1.7 reshape.143.refs_7_
  14.6 0.7 fusion.2
  15.3 0.6 compare_select_fusion.refs_10_
  15.9 0.1 fusion.1
  16.0 0.9 copy.29
  16.9 124.3 %forward.1 = (bf16[512,768]{1,0:T(8,128)(2,1)}, f32[2,768]{1,0:T(2,128)}, bf16[768,128]{1,0:T(8,128)(2,1)}, bf16[512,768]{1,0:T(8,128)(2,1)}, f32[512,1]{1,0:T(8...) custom-call(bf16[8,768]{1,0:T(8,128)(2,1)} %maximum_maximum_fusion.r, ...), custom_call_target="tpu_custom_call" | custom-call | tf_op jit(solution)/shard_map/forward/pallas_call | solution.py:558
  141.2 125.0 %backward.1 = (f32[576,128]{1,0:T(8,128)}, f32[576,128]{1,0:T(8,128)}, f32[144,128]{1,0:T(8,128)}, f32[432,128]{1,0:T(8,128)}, f32[144,128]{1,0:T(8,128)}, /*ind...) custom-call(bf16[512,768]{1,0:T(8,128)(2,1)} %bitcast.36, f32[512,1]{1,0:T(8,128)} %bitcast.38, ...), custom_call_target="tpu_custom_call" | custom-call | tf_op jit(solution)/shard_map/backward/pallas_call | solution.py:976
  266.2 0.0 copy-start.4
  266.3 0.0 copy-start.6
  266.3 0.0 copy-start.3
  266.3 0.9 reshape.161
  267.2 0.7 dynamic_slice.3
  267.8 2.1 copy.39
  270.0 2.7 copy.40
  272.6 0.7 copy.41
  273.3 0.6 copy.42
  274.0 0.7 copy.43
  274.7 0.6 copy.44
  275.3 0.7 copy.45
  276.1 0.7 copy.46
  276.8 0.9 copy.47
  (17 shorter events, 0.1 us)
Async XLA Ops:
  266.2 6.4 %copy-start.4 = (f32[432,128]{1,0:T(8,128)S(1)}, f32[432,128]{1,0:T(8,128)}, u32[]{:S(2)}) copy-start(f32[432,128]{1,0:T(8,128)} %get-tuple-element.78) | copy-start | bytes 663556
  266.3 7.1 %copy-start.6 = (f32[144,128]{1,0:T(8,128)S(1)}, f32[144,128]{1,0:T(8,128)}, u32[]{:S(2)}) copy-start(f32[144,128]{1,0:T(8,128)} %get-tuple-element.79) | copy-start | bytes 221188
  266.3 7.7 %copy-start.3 = (f32[432,128]{1,0:T(8,128)S(1)}, f32[432,128]{1,0:T(8,128)}, u32[]{:S(2)}) copy-start(f32[432,128]{1,0:T(8,128)} %get-tuple-element.80) | copy-start | bytes 663556
  266.3 8.4 %copy-start.5 = (f32[144,128]{1,0:T(8,128)S(1)}, f32[144,128]{1,0:T(8,128)}, u32[]{:S(2)}) copy-start(f32[144,128]{1,0:T(8,128)} %get-tuple-element.81) | copy-start | bytes 221188
  266.3 9.0 %copy-start.2 = (f32[576,128]{1,0:T(8,128)S(1)}, f32[576,128]{1,0:T(8,128)}, u32[]{:S(2)}) copy-start(f32[576,128]{1,0:T(8,128)} %get-tuple-element.82) | copy-start | bytes 884740
  267.8 8.2 %copy-start.1 = (f32[576,128]{1,0:T(8,128)S(1)}, f32[576,128]{1,0:T(8,128)}, u32[]{:S(2)}) copy-start(f32[576,128]{1,0:T(8,128)} %get-tuple-element.83) | copy-start | bytes 884740
  267.8 9.0 %copy-start = (f32[1296,128]{1,0:T(8,128)S(1)}, f32[1296,128]{1,0:T(8,128)}, u32[]{:S(2)}) copy-start(f32[1296,128]{1,0:T(8,128)} %get-tuple-element.84) | copy-start | bytes 1990660
